TPU v7x, 128 devices: a whole 4x4x4 slice. The times are simulated.
128 devices in a mesh: cand: 16 (over z_lo, y, core), rel: 8 (over z_hi, x).
Axes of the slice: x: 4, y: 4, z: 4 (z_hi: 2, z_lo: 2; z = z_hi * 2 + z_lo), core: 2. Of those that a mesh axis runs over, the one named last changes fastest.
Arguments:
- source_rows: bfloat16 [262144, 512], P(('cand', 'rel')), may hold values from -24 to 24
- rel_ids: int32 [262144, 1], P(('cand', 'rel')), may hold values from 0 to 15; in each aligned block of 2048 rows (0 to 2047, 2048 to 4095, ...) at most 256 rows name the same one
- relations: bfloat16 [16, 512, 512], P('rel'), may hold values from -0.25 to 0.25
- entities: float32 [32768, 512], P(('cand', 'rel')), may hold values from -0.3 to 0.3
- pos_slot: int32 [262144], P(('cand', 'rel')), may hold values from 0 to 2047
- negatives: int32 [8, 262144, 16], P(None, ('cand', 'rel')), may hold values from 0 to 255
Outputs:
- updated_entities: float32 [32768, 512], P(('cand', 'rel'))
- source_grad: bfloat16 [262144, 512], P(('cand', 'rel'))
- relation_grad: float32 [512, 16, 512], P('cand', 'rel')
Inputs may be any that keep to these rules, and one draw needn't show every extreme that they name: `rel_ids`: in each aligned block of 2048 rows (the rows of one device) no relation is named by more than 256 rows, a bound that some block reaches.
All inputs are finite; a program needn't handle non-finite values.
Results may differ from a plain program's by a relative error of at most 0.019.
Values may be sent and summed in bfloat16 or wider, within the bound.
A program may use at most 128 MiB of HBM per device.

v0:
```python
import jax
import jax.numpy as jnp
from jax import lax
from jax.sharding import PartitionSpec as P

STOPS = 8


learn_rate = 0.005


def from_behind(block, axis, distance):
    devices = range(lax.axis_size(axis))
    route = [((i - distance) % len(devices), i) for i in devices]
    return lax.ppermute(block, axis, route)


def slot_index(rel_ids, nrel, most):
    ids = rel_ids[:, 0]
    onehot = (ids[:, None] == jnp.arange(nrel, dtype=jnp.int32)[None, :]).astype(jnp.int32)
    rank = jnp.cumsum(onehot, axis=0) - onehot
    return ids * most + jnp.sum(rank * onehot, axis=1)


def place_rows(rows, slot, total):
    return jnp.zeros((total, rows.shape[1]), rows.dtype).at[slot].set(rows)


def shards(source_rows, rel_ids, relations, entities, pos_slot, negatives):
    src_rows, width = source_rows.shape
    rel_dev = relations.shape[0]
    owners = lax.axis_size("rel")
    nrel = rel_dev * owners
    most = 2 * src_rows // nrel
    slot = slot_index(rel_ids, nrel, most)
    sent = place_rows(source_rows, slot, nrel * most).reshape(nrel, most, width)
    every_matrix = lax.all_gather(relations, "rel", axis=0, tiled=True)
    q_slots = jnp.einsum(
        "kmd,kde->kme", sent, every_matrix, preferred_element_type=jnp.float32
    ).astype(jnp.bfloat16)
    queries = q_slots.reshape(nrel * most, width)[slot]
    part_rows = entities.shape[0]
    columns = jnp.arange(part_rows, dtype=jnp.int32)
    state = entities
    query_acc = jnp.zeros((src_rows, width), jnp.float32)
    for stop in range(STOPS):
        if stop > 0:
            state = from_behind(state, "cand", 1)
        wide = state.astype(jnp.bfloat16)
        logits = lax.dot_general(
            queries, wide, (((1,), (1,)), ((), ())), preferred_element_type=jnp.float32
        )
        picks = negatives[stop]
        counts = jnp.zeros(logits.shape, jnp.float32)
        for sample in range(picks.shape[1]):
            counts = counts + (picks[:, sample][:, None] == columns[None, :]).astype(jnp.float32)
        hits = (pos_slot[:, None] == stop * part_rows + columns[None, :]).astype(jnp.float32)
        weight = (counts * jax.nn.sigmoid(logits) - hits * jax.nn.sigmoid(-logits)).astype(
            jnp.bfloat16
        )
        query_acc = query_acc + jnp.dot(weight, wide, preferred_element_type=jnp.float32)
        change = lax.dot_general(
            weight, queries, (((0,), (0,)), ((), ())), preferred_element_type=jnp.float32
        )
        state = state - learn_rate * change
    query_grad = query_acc.astype(jnp.bfloat16)
    gq_slots = place_rows(query_grad, slot, nrel * most).reshape(nrel, most, width)
    back_slots = jnp.einsum(
        "kme,kde->kmd", gq_slots, every_matrix, preferred_element_type=jnp.float32
    ).astype(jnp.bfloat16)
    terms = jnp.einsum("kmd,kme->dke", sent, gq_slots, preferred_element_type=jnp.float32)
    partial_value = lax.psum_scatter(
        terms.astype(jnp.bfloat16), "rel", scatter_dimension=1, tiled=True
    )
    source_grad = back_slots.reshape(nrel * most, width)[slot]
    relation_grad = lax.psum_scatter(partial_value, "cand", scatter_dimension=0, tiled=True).astype(
        jnp.float32
    )
    return (state, source_grad, relation_grad)


def solution(mesh):
    placed = (
        P(("cand", "rel"), None),
        P(("cand", "rel"), None),
        P("rel", None, None),
        P(("cand", "rel"), None),
        P(("cand", "rel")),
        P(None, ("cand", "rel"), None),
    )
    return jax.shard_map(
        shards,
        mesh=mesh,
        in_specs=placed,
        out_specs=(P(("cand", "rel"), None), P(("cand", "rel"), None), P("cand", "rel", None)),
        check_vma=False,
    )
```

profile of v0, /device:TPU:0, one launch (start us, length us, event | category | flops | bytes accessed | tf_op | source)
XLA Modules:
  0.0 534.6 jit_solution(7300290726071133954)
XLA Ops:
  8.7 4.6 reduce-window.6
  15.4 12.6 %scatter_custom_fusion = bf16[4096,512]{1,0:T(8,128)(2,1)} fusion(s32[2048]{0:T(1024)S(1)} %bitcast.221, bf16[2048,512]{1,0:T(8,128)(2,1)} %param.6, bf16[]{:T(256)} %constant.14.clone.1), kind=kCustom, calls=%fused_computation.131 | custom fusion | bytes 4194816 | tf_op jit(solution)/shard_map/scatter | solution.py:26
  32.4 88.9 %all-gather.2.cloned.1.call-done = bf16[16,512,512]{2,1,0:T(8,128)(2,1)} async-done(((bf16[2,512,512]{2,1,0:T(8,128)(2,1)}), bf16[16,512,512]{2,1,0:T(8,128)(2,1)}) %all-gather.2.cloned.1.call-update) | async-done | bytes 8388624 | tf_op jit(solution)/shard_map/all_gather | solution.py:37
  121.3 9.2 %convolution_convert_fusion.1 = bf16[16,256,512]{2,1,0:T(8,128)(2,1)} fusion(bf16[16,256,512]{2,1,0:T(8,128)(2,1)} %bitcast.213, bf16[16,512,512]{2,1,0:T(8,128)(2,1)} %all-gather.2.cloned.1.call-done), kind=kOutput, calls=%fused_computation.7 | convolution fusion | flops 2149580800 | bytes 16777216 | tf_op jit(solution)/shard_map/kmd,kde->kme/dot_general | solution.py:38
  130.4 10.4 %gather_fusion = bf16[2048,512]{1,0:T(8,128)(2,1)S(1)} fusion(bf16[4096,512]{1,0:T(8,128)(2,1)} %bitcast.211, s32[2048]{0:T(1024)S(1)} %broadcast_clamp_fusion), kind=kCustom, calls=%fused_computation | custom fusion | bytes 4202496 | tf_op jit(solution)/shard_map/gather | solution.py:41
  140.8 5.2 subtract_convert_fusion.7
  147.3 10.6 %collective-permute-done = f32[256,512]{1,0:T(8,128)S(1)} collective-permute-done((f32[256,512]{1,0:T(8,128)S(1)}, f32[256,512]{1,0:T(8,128)S(1)}, u32[]{:S(2)}, u32[]{:S(2)}) %collective-permute-start) | collective-permute-done | bytes 524320 | tf_op jit(solution)/shard_map/ppermute | solution.py:15
  158.1 5.2 subtract_convert_fusion.6
  164.4 10.6 %collective-permute-done.1 = f32[256,512]{1,0:T(8,128)S(1)} collective-permute-done((f32[256,512]{1,0:T(8,128)S(1)}, f32[256,512]{1,0:T(8,128)S(1)}, u32[]{:S(2)}, u32[]{:S(2)}) %collective-permute-start.1) | collective-permute-done | bytes 524320 | tf_op jit(solution)/shard_map/ppermute | solution.py:15
  175.1 5.2 subtract_convert_fusion.5
  181.4 10.6 %collective-permute-done.2 = f32[256,512]{1,0:T(8,128)S(1)} collective-permute-done((f32[256,512]{1,0:T(8,128)S(1)}, f32[256,512]{1,0:T(8,128)S(1)}, u32[]{:S(2)}, u32[]{:S(2)}) %collective-permute-start.2) | collective-permute-done | bytes 524320 | tf_op jit(solution)/shard_map/ppermute | solution.py:15
  192.1 5.2 subtract_convert_fusion.4
  198.3 2.8 fusion.57
  201.1 7.7 %collective-permute-done.3 = f32[256,512]{1,0:T(8,128)S(1)} collective-permute-done((f32[256,512]{1,0:T(8,128)S(1)}, f32[256,512]{1,0:T(8,128)S(1)}, u32[]{:S(2)}, u32[]{:S(2)}) %collective-permute-start.3) | collective-permute-done | bytes 524320 | tf_op jit(solution)/shard_map/ppermute | solution.py:15
  209.0 5.2 subtract_convert_fusion.3
  217.9 2.8 fusion.45
  220.7 5.3 collective-permute-done.4
  225.9 5.2 subtract_convert_fusion.2
  231.9 2.7 fusion.39
  234.6 2.8 fusion.33
  237.4 5.2 collective-permute-done.5
  242.6 5.1 subtract_convert_fusion.1
  251.5 2.8 fusion.21
  254.3 5.3 collective-permute-done.6
  259.5 5.2 subtract_convert_fusion
  267.4 17.9 %scatter_custom_fusion.1 = bf16[4096,512]{1,0:T(8,128)(2,1)} fusion(s32[2048]{0:T(1024)} %bitcast.223, f32[2048,512]{1,0:T(8,128)} %fusion.15, f32[2048,512]{1,0:T(8,128)} %fusion.21, f32[2048,512]{1,0:T(8,128)} %fusion.27, f32[2048,512]{1,0:T(8,128)} %fusion.33, f32[2048,512]{1,0:T(8,128)} %fusion.39, f32[2048,512]{1,0:T(8,128)} %fusion.45, ...), kind=kCustom, calls=%fused_computation.8 | custom fusion | flops 8388608 | bytes 37749248 | tf_op jit(solution)/shard_map/scatter | solution.py:26
  285.3 9.1 %convert_bitcast_fusion = bf16[512,16,512]{0,2,1:T(8,128)(2,1)} fusion(bf16[16,256,512]{2,1,0:T(8,128)(2,1)} %bitcast.215, bf16[16,256,512]{2,1,0:T(8,128)(2,1)} %bitcast.214), kind=kOutput, calls=%fused_computation.4 | convolution fusion | flops 2151677952 | bytes 16777216 | tf_op jit(solution)/shard_map/kmd,kme->dke/dot_general | solution.py:71
  296.3 108.0 %reduce-scatter.2.cloned.1.call-done = bf16[512,2,512]{0,2,1:T(8,128)(2,1)} async-done(((bf16[512,16,512]{0,2,1:T(8,128)(2,1)}), bf16[512,2,512]{0,2,1:T(8,128)(2,1)}) %reduce-scatter.2.cloned.1.call-update) | async-done | bytes 1048592 | tf_op jit(solution)/shard_map/reduce_scatter | solution.py:72
  404.4 3.7 copy.14
  408.1 9.2 %convolution_convert_fusion = bf16[16,256,512]{2,1,0:T(8,128)(2,1)} fusion(bf16[16,256,512]{2,1,0:T(8,128)(2,1)} %bitcast.216, bf16[16,512,512]{2,1,0:T(8,128)(2,1)} %all-gather.2.cloned.1.call-done), kind=kOutput, calls=%fused_computation.6 | convolution fusion | flops 2149580800 | bytes 16777216 | tf_op jit(solution)/shard_map/kme,kde->kmd/dot_general | solution.py:68
  417.2 12.0 %gather_fusion.1 = bf16[2048,512]{1,0:T(8,128)(2,1)} fusion(bf16[4096,512]{1,0:T(8,128)(2,1)} %bitcast.212, s32[2048]{0:T(1024)S(1)} %copy-done.4), kind=kCustom, calls=%fused_computation.1 | custom fusion | bytes 4202496 | tf_op jit(solution)/shard_map/gather | solution.py:75
  431.8 94.3 %all-reduce.3.cloned.1.call-done = bf16[512,2,512]{2,1,0:T(2,128)(2,1)} async-done(((bf16[512,2,512]{2,1,0:T(2,128)(2,1)}), bf16[512,2,512]{2,1,0:T(2,128)(2,1)}) %all-reduce.3.cloned.1.call-update) | async-done | bytes 1048592
  (197 shorter events, 28.1 us)
Async XLA Ops:
  7.2 114.1 %all-gather.2.cloned.1.call-start = ((), (), s32[]{:S(2)}) async-start(), calls=%async_computation.1 | async-start | bytes 9437184 | tf_op jit(solution)/shard_map/all_gather | solution.py:37
  7.9 396.5 %reduce-scatter.2.cloned.1.call-start = ((), (), s32[]{:S(2)}) async-start(), calls=%async_computation.2 | async-start | bytes 9437184 | tf_op jit(solution)/shard_map/reduce_scatter | solution.py:72
  15.4 13.8 %copy-start.5 = (s32[2048,1]{0,1:T(1,128)}, s32[2048,1]{0,1:T(1,128)S(1)}, u32[]{:S(2)}) copy-start(s32[2048,1]{0,1:T(1,128)S(1)} %compare_select_fusion) | copy-start | bytes 24580
  15.4 13.8 %copy-start = (s32[8,2048,16]{1,2,0:T(8,128)S(1)}, s32[8,2048,16]{1,2,0:T(8,128)}, u32[]{:S(2)}) copy-start(s32[8,2048,16]{1,2,0:T(8,128)} %param.11) | copy-start | bytes 3145732
  29.2 101.2 %copy-start.3 = (s32[2048]{0:T(1024)}, s32[2048]{0:T(1024)S(1)}, u32[]{:S(2)}) copy-start(s32[2048]{0:T(1024)S(1)} %broadcast_clamp_fusion) | copy-start | bytes 24580
  146.1 11.9 %copy-start.53 = (s32[2048,1]{0,1:T(1,128)S(1)}, s32[2048,1]{0,1:T(1,128)}, u32[]{:S(2)}) copy-start(s32[2048,1]{0,1:T(1,128)} %get-tuple-element.113) | copy-start | bytes 24580
  146.1 11.9 %copy-start.54 = (s32[2048,1]{0,1:T(1,128)S(1)}, s32[2048,1]{0,1:T(1,128)}, u32[]{:S(2)}) copy-start(s32[2048,1]{0,1:T(1,128)} %get-tuple-element.114) | copy-start | bytes 24580
  146.1 11.9 %copy-start.55 = (s32[2048,1]{0,1:T(1,128)S(1)}, s32[2048,1]{0,1:T(1,128)}, u32[]{:S(2)}) copy-start(s32[2048,1]{0,1:T(1,128)} %get-tuple-element.115) | copy-start | bytes 24580
  146.1 11.9 %copy-start.56 = (s32[2048,1]{0,1:T(1,128)S(1)}, s32[2048,1]{0,1:T(1,128)}, u32[]{:S(2)}) copy-start(s32[2048,1]{0,1:T(1,128)} %get-tuple-element.116) | copy-start | bytes 24580
  146.1 11.9 %copy-start.57 = (s32[2048,1]{0,1:T(1,128)S(1)}, s32[2048,1]{0,1:T(1,128)}, u32[]{:S(2)}) copy-start(s32[2048,1]{0,1:T(1,128)} %get-tuple-element.117) | copy-start | bytes 24580
  146.1 11.9 %copy-start.58 = (s32[2048,1]{0,1:T(1,128)S(1)}, s32[2048,1]{0,1:T(1,128)}, u32[]{:S(2)}) copy-start(s32[2048,1]{0,1:T(1,128)} %get-tuple-element.118) | copy-start | bytes 24580
  146.1 11.9 %copy-start.59 = (s32[2048,1]{0,1:T(1,128)S(1)}, s32[2048,1]{0,1:T(1,128)}, u32[]{:S(2)}) copy-start(s32[2048,1]{0,1:T(1,128)} %get-tuple-element.119) | copy-start | bytes 24580
  146.1 11.9 %copy-start.60 = (s32[2048,1]{0,1:T(1,128)S(1)}, s32[2048,1]{0,1:T(1,128)}, u32[]{:S(2)}) copy-start(s32[2048,1]{0,1:T(1,128)} %get-tuple-element.120) | copy-start | bytes 24580
  146.1 11.9 %copy-start.61 = (s32[2048,1]{0,1:T(1,128)S(1)}, s32[2048,1]{0,1:T(1,128)}, u32[]{:S(2)}) copy-start(s32[2048,1]{0,1:T(1,128)} %get-tuple-element.121) | copy-start | bytes 24580
  146.1 11.9 %copy-start.62 = (s32[2048,1]{0,1:T(1,128)S(1)}, s32[2048,1]{0,1:T(1,128)}, u32[]{:S(2)}) copy-start(s32[2048,1]{0,1:T(1,128)} %get-tuple-element.122) | copy-start | bytes 24580
  146.2 11.9 %copy-start.63 = (s32[2048,1]{0,1:T(1,128)S(1)}, s32[2048,1]{0,1:T(1,128)}, u32[]{:S(2)}) copy-start(s32[2048,1]{0,1:T(1,128)} %get-tuple-element.123) | copy-start | bytes 24580
  146.2 11.9 %copy-start.64 = (s32[2048,1]{0,1:T(1,128)S(1)}, s32[2048,1]{0,1:T(1,128)}, u32[]{:S(2)}) copy-start(s32[2048,1]{0,1:T(1,128)} %get-tuple-element.124) | copy-start | bytes 24580
  146.2 11.9 %copy-start.65 = (s32[2048,1]{0,1:T(1,128)S(1)}, s32[2048,1]{0,1:T(1,128)}, u32[]{:S(2)}) copy-start(s32[2048,1]{0,1:T(1,128)} %get-tuple-element.125) | copy-start | bytes 24580
  146.2 11.9 %copy-start.66 = (s32[2048,1]{0,1:T(1,128)S(1)}, s32[2048,1]{0,1:T(1,128)}, u32[]{:S(2)}) copy-start(s32[2048,1]{0,1:T(1,128)} %get-tuple-element.126) | copy-start | bytes 24580
  146.2 11.9 %copy-start.67 = (s32[2048,1]{0,1:T(1,128)S(1)}, s32[2048,1]{0,1:T(1,128)}, u32[]{:S(2)}) copy-start(s32[2048,1]{0,1:T(1,128)} %get-tuple-element.127) | copy-start | bytes 24580
  146.2 11.9 %copy-start.68 = (s32[2048,1]{0,1:T(1,128)S(1)}, s32[2048,1]{0,1:T(1,128)}, u32[]{:S(2)}) copy-start(s32[2048,1]{0,1:T(1,128)} %get-tuple-element.128) | copy-start | bytes 24580
  146.2 11.9 %copy-start.70 = (s32[2048]{0:T(1024)S(1)}, s32[2048]{0:T(1024)}, u32[]{:S(2)}) copy-start(s32[2048]{0:T(1024)} %param.10) | copy-start | bytes 24580
  146.2 11.9 %copy-start.73 = (s32[256]{0:T(256)S(1)}, s32[256]{0:T(256)}, u32[]{:S(2)}) copy-start(s32[256]{0:T(256)} %iota_add_fusion.6) | copy-start | bytes 3076
  147.0 11.0 %collective-permute-start = (f32[256,512]{1,0:T(8,128)S(1)}, f32[256,512]{1,0:T(8,128)S(1)}, u32[]{:S(2)}, u32[]{:S(2)}) collective-permute-start(f32[256,512]{1,0:T(8,128)S(1)} %fusion.11), channel_id=1, source_target_pairs={{120,0},{0,8},{8,16},{16,24},{24,32},{32,40},{40,48},{48,56},{56,6... | collective-permute-start | bytes 1572872 | tf_op jit(solution)/shard_map/ppermute | solution.py:15
  163.3 11.7 %copy-start.37 = (s32[2048,1]{0,1:T(1,128)S(1)}, s32[2048,1]{0,1:T(1,128)}, u32[]{:S(2)}) copy-start(s32[2048,1]{0,1:T(1,128)} %get-tuple-element.97) | copy-start | bytes 24580
  164.2 10.8 %collective-permute-start.1 = (f32[256,512]{1,0:T(8,128)S(1)}, f32[256,512]{1,0:T(8,128)S(1)}, u32[]{:S(2)}, u32[]{:S(2)}) collective-permute-start(f32[256,512]{1,0:T(8,128)S(1)} %fusion.10), channel_id=1, source_target_pairs={{120,0},{0,8},{8,16},{16,24},{24,32},{32,40},{40,48},{48,56},{56,6... | collective-permute-start | bytes 1572872 | tf_op jit(solution)/shard_map/ppermute | solution.py:15
  181.2 10.8 %collective-permute-start.2 = (f32[256,512]{1,0:T(8,128)S(1)}, f32[256,512]{1,0:T(8,128)S(1)}, u32[]{:S(2)}, u32[]{:S(2)}) collective-permute-start(f32[256,512]{1,0:T(8,128)S(1)} %fusion.9), channel_id=1, source_target_pairs={{120,0},{0,8},{8,16},{16,24},{24,32},{32,40},{40,48},{48,56},{56,6... | collective-permute-start | bytes 1572872 | tf_op jit(solution)/shard_map/ppermute | solution.py:15
  198.1 10.8 %collective-permute-start.3 = (f32[256,512]{1,0:T(8,128)S(1)}, f32[256,512]{1,0:T(8,128)S(1)}, u32[]{:S(2)}, u32[]{:S(2)}) collective-permute-start(f32[256,512]{1,0:T(8,128)S(1)} %fusion.8), channel_id=1, source_target_pairs={{120,0},{0,8},{8,16},{16,24},{24,32},{32,40},{40,48},{48,56},{56,6... | collective-permute-start | bytes 1572872 | tf_op jit(solution)/shard_map/ppermute | solution.py:15
  214.9 11.0 %collective-permute-start.4 = (f32[256,512]{1,0:T(8,128)S(1)}, f32[256,512]{1,0:T(8,128)S(1)}, u32[]{:S(2)}, u32[]{:S(2)}) collective-permute-start(f32[256,512]{1,0:T(8,128)S(1)} %fusion.7), channel_id=1, source_target_pairs={{120,0},{0,8},{8,16},{16,24},{24,32},{32,40},{40,48},{48,56},{56,6... | collective-permute-start | bytes 1572872 | tf_op jit(solution)/shard_map/ppermute | solution.py:15
  231.8 10.8 %collective-permute-start.5 = (f32[256,512]{1,0:T(8,128)S(1)}, f32[256,512]{1,0:T(8,128)S(1)}, u32[]{:S(2)}, u32[]{:S(2)}) collective-permute-start(f32[256,512]{1,0:T(8,128)S(1)} %fusion.6), channel_id=1, source_target_pairs={{120,0},{0,8},{8,16},{16,24},{24,32},{32,40},{40,48},{48,56},{56,6... | collective-permute-start | bytes 1572872 | tf_op jit(solution)/shard_map/ppermute | solution.py:15
  248.5 11.0 %collective-permute-start.6 = (f32[256,512]{1,0:T(8,128)S(1)}, f32[256,512]{1,0:T(8,128)S(1)}, u32[]{:S(2)}, u32[]{:S(2)}) collective-permute-start(f32[256,512]{1,0:T(8,128)S(1)} %fusion.5), channel_id=1, source_target_pairs={{120,0},{0,8},{8,16},{16,24},{24,32},{32,40},{40,48},{48,56},{56,6... | collective-permute-start | bytes 1572872 | tf_op jit(solution)/shard_map/ppermute | solution.py:15
  294.5 231.6 %all-reduce.3.cloned.1.call-start = ((), (), s32[]{:S(2)}) async-start(), calls=%async_computation.3 | async-start | bytes 2097152
  (52 other events, 569.2 us)
Sparse Core Ops, SparseCore 0:
  10.3 110.9 all-gather.1
  294.6 109.7 reduce-scatter.1
  408.2 117.8 all-reduce.2
where the time goes:
time: 544 us; the launch traced here: 535 us
  waiting for transfers between devices  347 us (64%)
  matrix products  98.3 us (18%)
  local copies, waits for them, and re-layouts  43.7 us (8%)
  other arithmetic  27.7 us (5%)
  between operations  16.2 us (3%)
    reduce_scatter x1, waiting for transfers between devices, shards(): lax.psum_scatter(terms.astype(jnp.bfloat16), 'rel', scatter_dimension=1,...  108 us
    unnamed x4, waiting for transfers between devices  95 us
    all_gather x1, waiting for transfers between devices, shards(): every_matrix = lax.all_gather(relations, 'rel', axis=0, tiled=True)  88.9 us
    ppermute x7, waiting for transfers between devices, from_behind(): return lax.ppermute(block, axis, route)  55.3 us
    dot_general x8, matrix products, shards(): lax.dot_general(queries, wide, (((1,), (1,)), ((), ())), preferred_elemen...  41.4 us
    dot_general x8, matrix products, shards(): jnp.dot(weight, wide, preferred_element_type=jnp.float32)  21.8 us
    scatter x1, other arithmetic, place_rows(): return jnp.zeros((total, rows.shape[1]), rows.dtype).at[slot].set(rows)  17.9 us
    scatter x1, local copies, waits for them, and re-layouts, place_rows(): return jnp.zeros((total, rows.shape[1]), rows.dtype).at[slot].set(rows)  12.6 us
  transfers between devices with their start and end apart: 10, of which 10 were waited for; matrix products, arithmetic and copies ran while one was open for 13% of the time, Pallas kernels for 0%

commit v1 on v0

v1 whole, which is shorter than its diff:
```python
import functools

import jax
import jax.numpy as jnp
from jax import lax
from jax.experimental import pallas as pl
from jax.experimental.pallas import tpu as pltpu
from jax.sharding import PartitionSpec as P

MESH = pl.DeviceIdType.MESH
BF = jnp.bfloat16
F32 = jnp.float32


class Spot:
    def __init__(self):
        cand, rel = lax.axis_index("cand"), lax.axis_index("rel")
        self.core = lax.rem(cand, 2)
        self.y = lax.rem(cand // 2, 4)
        self.zl = cand // 8
        self.x = lax.rem(rel, 4)
        self.zh = rel // 4
        self.z = self.zh * 2 + self.zl
        self.rel = rel

    def device(self, x=None, y=None, z=None, core=None):
        x = self.x if x is None else x
        y = self.y if y is None else y
        z = self.z if z is None else z
        core = self.core if core is None else core
        return ((lax.rem(z, 2) * 4 + y) * 2 + core, (z // 2) * 4 + x)


def turn(i, by):
    return lax.rem(i + by, 4)


def greet(devices):
    barrier = pltpu.get_barrier_semaphore()
    for device in devices:
        pl.semaphore_signal(barrier, inc=1, device_id=device, device_id_type=MESH)
    pl.semaphore_wait(barrier, len(devices))


class Mail:
    def __init__(self, send_sem, recv_sem):
        self.send_sem, self.recv_sem, self.count, self.sent = send_sem, recv_sem, 0, []

    def send(self, src, dst, device):
        i = self.count
        self.count += 1
        copy = pltpu.make_async_remote_copy(
            src_ref=src,
            dst_ref=dst,
            send_sem=self.send_sem.at[i],
            recv_sem=self.recv_sem.at[i],
            device_id=device,
            device_id_type=MESH,
        )
        copy.start()
        self.sent.append(copy)
        return copy

    def drain(self):
        for copy in self.sent:
            copy.wait_send()


def gather_kernel(own, out, local_sem, send_sem, recv_sem):
    at = Spot()
    mail = Mail(send_sem, recv_sem)
    left, right = at.device(x=turn(at.x, 3)), at.device(x=turn(at.x, 1))
    across = at.device(z=3 - at.z)
    partner = at.device(core=1 - at.core)
    greet([left, right, across, partner])
    here = pltpu.make_async_copy(own, out.at[at.rel], local_sem)
    here.start()
    half = own.shape[1] // 2
    start = pl.multiple_of(at.core * half, half)
    mine = pl.ds(start, half)
    first = pl.ds(start, half // 2)
    second = pl.ds(pl.multiple_of(start + half // 2, half // 2), half // 2)
    me, far = at.zh * 4, (1 - at.zh) * 4
    x0, x1, x2, x3 = at.x, turn(at.x, 1), turn(at.x, 2), turn(at.x, 3)
    own_mine = own.at[:, mine]

    def block(base, x, rows):
        return out.at[base + x, :, rows]

    to_across = mail.send(own_mine, block(me, x0, mine), across)
    to_right = mail.send(own_mine, block(me, x0, mine), right)
    to_left = mail.send(own_mine, block(me, x0, mine), left)
    to_right.wait_recv()
    on_right = mail.send(block(me, x3, first), block(me, x3, first), right)
    share = [mail.send(block(me, x3, mine), block(me, x3, mine), partner)]
    to_left.wait_recv()
    on_left = mail.send(block(me, x1, second), block(me, x1, second), left)
    share.append(mail.send(block(me, x1, mine), block(me, x1, mine), partner))
    to_across.wait_recv()
    far_right = mail.send(block(far, x0, mine), block(far, x0, mine), right)
    far_left = mail.send(block(far, x0, mine), block(far, x0, mine), left)
    share.append(mail.send(block(far, x0, mine), block(far, x0, mine), partner))
    on_right.wait_recv()
    opposite_a = mail.send(block(me, x2, first), block(me, x2, first), across)
    on_left.wait_recv()
    opposite_b = mail.send(block(me, x2, second), block(me, x2, second), across)
    share.append(mail.send(block(me, x2, mine), block(me, x2, mine), partner))
    far_right.wait_recv()
    share.append(mail.send(block(far, x3, mine), block(far, x3, mine), partner))
    far_left.wait_recv()
    share.append(mail.send(block(far, x1, mine), block(far, x1, mine), partner))
    opposite_a.wait_recv()
    opposite_b.wait_recv()
    share.append(mail.send(block(far, x2, mine), block(far, x2, mine), partner))
    for copy in share:
        copy.wait_recv()
    mail.drain()
    here.wait()


def gather_relations(relations):
    per, width, _ = relations.shape
    owners = lax.axis_size("rel")
    out = pl.pallas_call(
        gather_kernel,
        out_shape=jax.ShapeDtypeStruct((owners, per, width, width), relations.dtype),
        in_specs=[pl.BlockSpec(memory_space=pltpu.VMEM)],
        out_specs=pl.BlockSpec(memory_space=pl.ANY),
        scratch_shapes=[
            pltpu.SemaphoreType.DMA,
            pltpu.SemaphoreType.DMA((20,)),
            pltpu.SemaphoreType.DMA((20,)),
        ],
        compiler_params=pltpu.CompilerParams(collective_id=0, has_side_effects=True),
        name="gather_relations",
    )(relations)
    return out.reshape(owners * per, width, width)


def add_into(dst, *others):
    lead = dst.shape[:-2]
    total = 1
    for n in lead:
        total *= n

    def body(i, carry):
        index, rest = [], i
        for n in reversed(lead):
            index.insert(0, lax.rem(rest, n))
            rest = rest // n
        value = dst[tuple(index)].astype(F32)
        for other in others:
            value = value + other[tuple(index)].astype(F32)
        dst[tuple(index)] = value.astype(dst.dtype)
        return carry

    lax.fori_loop(0, total, body, 0)


class Ring:
    def __init__(self, mail, place, ahead, behind, piece, halves, land_half, land_full):
        self.mail, self.place, self.ahead, self.behind = mail, place, ahead, behind
        self.piece, self.halves, self.land_half, self.land_full = piece, halves, land_half, land_full

    def one(self):
        far = turn(self.place, 2)
        self.h = [
            self.mail.send(self.halves(self.piece(far))[d], self.land_half[d], device)
            for d, device in enumerate((self.ahead, self.behind))
        ]

    def two(self):
        self.f = []
        for d, (step, device) in enumerate(((1, self.ahead), (3, self.behind))):
            self.h[d].wait_recv()
            target = self.piece(turn(self.place, step))
            add_into(self.halves(target)[d], self.land_half[d])
            self.f.append(self.mail.send(target, self.land_full[d], device))

    def three(self):
        for copy in self.f:
            copy.wait_recv()
        return self.piece(self.place), self.land_full


def scatter_kernel(
    terms, out, got, ax_h, ax_f, ay_h, ay_f, az_h, az_f, by_h, by_f, bx_h, bx_f, bz_h, bz_f, send_sem, recv_sem
):
    at = Spot()
    mail = Mail(send_sem, recv_sem)
    partner = at.device(core=1 - at.core)
    xs = at.device(x=turn(at.x, 1)), at.device(x=turn(at.x, 3))
    ys = at.device(y=turn(at.y, 1)), at.device(y=turn(at.y, 3))
    zs = at.device(z=turn(at.z, 1)), at.device(z=turn(at.z, 3))
    greet([partner, *xs, *ys, *zs])

    swap = [mail.send(terms.at[j, :, :, :, :, 1 - at.core], got.at[j], partner) for j in range(2)]

    def first_half(ref):
        return ref.at[0], ref.at[1]

    def row_halves(ref):
        rows = ref.shape[0] // 2
        return ref.at[pl.ds(0, rows)], ref.at[pl.ds(rows, rows)]

    def two(ref):
        return ref.at[0], ref.at[1]

    a, b = got.at[0], got.at[1]
    ax = Ring(mail, at.x, *xs, lambda t: a.at[:, t], first_half, two(ax_h), two(ax_f))
    a1 = lambda: a.at[:, at.x]
    ay = Ring(mail, at.y, *ys, lambda t: a1().at[:, :, t], first_half, two(ay_h), two(ay_f))
    a2 = lambda z: a.at[z // 2, at.x, lax.rem(z, 2), at.y]
    az = Ring(mail, at.z, *zs, a2, row_halves, two(az_h), two(az_f))
    by = Ring(mail, at.y, *ys, lambda t: b.at[:, :, :, t], first_half, two(by_h), two(by_f))
    bx = Ring(mail, at.x, *xs, lambda t: b.at[:, t, :, at.y], first_half, two(bx_h), two(bx_f))
    b2 = lambda z: b.at[z // 2, at.x, lax.rem(z, 2), at.y]
    bz = Ring(mail, at.z, *zs, b2, row_halves, two(bz_h), two(bz_f))

    for j, (ref, ring) in enumerate(((a, ax), (b, by))):
        swap[j].wait_recv()
        add_into(ref, terms.at[j, :, :, :, :, at.core])
        ring.one()
    ax.two()
    by.two()
    for ring, following in ((ax, ay), (by, bx)):
        piece, landed = ring.three()
        add_into(piece, *landed)
        following.one()
    ay.two()
    bx.two()
    for ring, following in ((ay, az), (bx, bz)):
        piece, landed = ring.three()
        add_into(piece, *landed)
        following.one()
    az.two()
    bz.two()
    for j, ring in enumerate((az, bz)):
        piece, landed = ring.three()
        out[:, j, :] = piece[...].astype(F32) + landed[0][...].astype(F32) + landed[1][...].astype(F32)
    mail.drain()


def scatter_terms(terms):
    nrel, width, _ = terms.shape
    rows = width // 16
    shaped = terms.reshape(2, 2, 4, 2, 4, 2, rows, width)
    v = lambda *lead: pltpu.VMEM((*lead, rows, width), BF)
    z = lambda r: pltpu.VMEM((2, r, width), BF)
    return pl.pallas_call(
        scatter_kernel,
        out_shape=jax.ShapeDtypeStruct((rows, 2, width), F32),
        in_specs=[pl.BlockSpec(memory_space=pltpu.VMEM)],
        out_specs=pl.BlockSpec(memory_space=pltpu.VMEM),
        scratch_shapes=[
            v(2, 2, 4, 2, 4),
            v(2, 2, 4), v(2, 2, 2, 4), v(2, 2), v(2, 2, 2), z(rows // 2), v(2),
            v(2, 4, 2), v(2, 2, 4, 2), v(2, 2), v(2, 2, 2), z(rows // 2), v(2),
            pltpu.SemaphoreType.DMA((26,)),
            pltpu.SemaphoreType.DMA((26,)),
        ],
        compiler_params=pltpu.CompilerParams(
            collective_id=1, has_side_effects=True, vmem_limit_bytes=60 << 20
        ),
        name="scatter_terms",
    )(shaped)

STOPS = 8
learn_rate = 0.005
LOW = 64


def stops_kernel(
    q, neg, pos, entities, state_out, grad_out,
    held, sent, wide, weights, acc, low, unit, packed, local_sem, send_sem, recv_sem,
):
    cand, rel = lax.axis_index("cand"), lax.axis_index("rel")
    n = lax.axis_size("cand")
    ahead, behind = (lax.rem(cand + 1, n), rel), (lax.rem(cand + n - 1, n), rel)
    greet([ahead, behind])
    part, width = entities.shape
    rows = q.shape[0]
    chunk = part // 2
    parts = part // LOW
    block = 256
    lanes = 128

    fetch = [
        pltpu.make_async_copy(entities.at[pl.ds(h * chunk, chunk)], held.at[h], local_sem.at[h])
        for h in range(2)
    ]
    for copy in fetch:
        copy.start()

    def tally(stop):
        picks = neg[stop]
        samples = picks.shape[0]
        low[0:samples, :] = lax.bitwise_and(picks, LOW - 1)
        unit[0:samples, :] = lax.shift_left(jnp.ones_like(picks), 8 * lax.shift_right_logical(picks, 6))
        place = pos[...] - stop * part
        inside = (place >= 0) & (place < part)
        place = jnp.where(inside, place, 0)
        low[samples : samples + 1, :] = lax.bitwise_and(place, LOW - 1)
        unit[samples : samples + 1, :] = jnp.where(
            inside, lax.shift_left(jnp.full_like(place, 32), 8 * lax.shift_right_logical(place, 6)), 0
        )

        def column(c, carry):
            here = pl.ds(pl.multiple_of(c * lanes, lanes), lanes)
            index = lax.broadcasted_iota(jnp.int32, (LOW, lanes), 0)
            total = jnp.zeros((LOW, lanes), jnp.int32)
            for k in range(samples + 1):
                match = jnp.broadcast_to(low[k : k + 1, here], (LOW, lanes)) == index
                total = total + jnp.where(match, jnp.broadcast_to(unit[k : k + 1, here], (LOW, lanes)), 0)
            packed[:, here] = total
            return carry

        lax.fori_loop(0, rows // lanes, column, 0)

    tally(0)
    acc[...] = jnp.zeros_like(acc)
    for copy in fetch:
        copy.wait()

    def hop(t):
        return pltpu.make_async_remote_copy(
            src_ref=sent.at[t],
            dst_ref=held.at[t + 2],
            send_sem=send_sem.at[t],
            recv_sem=recv_sem.at[t],
            device_id=ahead,
            device_id_type=MESH,
        )

    def step(t, carry):
        half = lax.rem(t, 2)
        base = half * chunk

        @pl.when(t >= 2)
        def _():
            hop(t - 2).wait_recv()

        state = held[t]
        rounded = state.astype(BF)
        wide[pl.ds(pl.multiple_of(base, chunk), chunk), :] = rounded
        pieces = []
        for i in range(rows // block):
            here = pl.ds(i * block, block)
            logits = lax.dot_general(
                rounded, q[here, :], (((1,), (1,)), ((), ())), preferred_element_type=F32
            )
            marks = packed[:, here]
            marks = jnp.concatenate(
                [
                    lax.bitwise_and(lax.shift_right_logical(marks, 16 * half + 8 * p), 63)
                    for p in range(chunk // LOW)
                ],
                axis=0,
            )
            count = lax.bitwise_and(marks, 31).astype(F32)
            small = jnp.exp(-jnp.abs(logits))
            big = 1.0 / (1.0 + small)
            small = small * big
            positive = logits >= 0
            up = count * jnp.where(positive, big, small)
            down = jnp.where(positive, small, big)
            pieces.append(jnp.where(marks >= 32, up - down, up).astype(BF))
        weight = jnp.concatenate(pieces, axis=1)
        weights[pl.ds(pl.multiple_of(base, chunk), chunk), :] = weight
        change = jnp.dot(weight, q[...], preferred_element_type=F32)
        sent[t] = state - learn_rate * change

        @pl.when(t < 2 * STOPS - 2)
        def _():
            hop(t).start()

        @pl.when(half == 1)
        def _():
            def gather(c, carry):
                here = pl.ds(pl.multiple_of(c * block, block), block)
                acc[:, here] += lax.dot_general(
                    wide[...], weights[:, here], (((0,), (0,)), ((), ())), preferred_element_type=F32
                )
                return carry

            lax.fori_loop(0, rows // block, gather, 0)

            @pl.when(t < 2 * STOPS - 1)
            def _():
                tally(t // 2 + 1)

        return carry

    lax.fori_loop(0, 2 * STOPS, step, 0)
    for h in range(2):
        state_out[pl.ds(h * chunk, chunk), :] = sent[2 * STOPS - 2 + h]

    def turned(c, carry):
        here = pl.ds(pl.multiple_of(c * block, block), block)
        grad_out[here, :] = acc[:, here].T.astype(BF)
        return carry

    lax.fori_loop(0, rows // block, turned, 0)

    def drained(t, carry):
        hop(t).wait_send()
        return carry

    lax.fori_loop(0, 2 * STOPS - 2, drained, 0)


def run_stops(queries, picks, pos, entities):
    rows, width = queries.shape
    part = entities.shape[0]
    chunk = part // 2
    vmem = pl.BlockSpec(memory_space=pltpu.VMEM)
    hops = 2 * STOPS
    return pl.pallas_call(
        stops_kernel,
        out_shape=(
            jax.ShapeDtypeStruct((part, width), F32),
            jax.ShapeDtypeStruct((rows, width), BF),
        ),
        in_specs=[vmem, vmem, vmem, pl.BlockSpec(memory_space=pl.ANY)],
        out_specs=(vmem, vmem),
        scratch_shapes=[
            pltpu.VMEM((hops, chunk, width), F32),
            pltpu.VMEM((hops, chunk, width), F32),
            pltpu.VMEM((part, width), BF),
            pltpu.VMEM((part, rows), BF),
            pltpu.VMEM((width, rows), F32),
            pltpu.VMEM((24, rows), jnp.int32),
            pltpu.VMEM((24, rows), jnp.int32),
            pltpu.VMEM((LOW, rows), jnp.int32),
            pltpu.SemaphoreType.DMA((2,)),
            pltpu.SemaphoreType.DMA((hops,)),
            pltpu.SemaphoreType.DMA((hops,)),
        ],
        compiler_params=pltpu.CompilerParams(
            collective_id=2, has_side_effects=True, vmem_limit_bytes=60 << 20
        ),
        name="run_stops",
    )(queries, picks, pos, entities)


def slot_index(rel_ids, nrel, most):
    ids = rel_ids[:, 0]
    onehot = (ids[:, None] == jnp.arange(nrel, dtype=jnp.int32)[None, :]).astype(jnp.int32)
    rank = jnp.cumsum(onehot, axis=0) - onehot
    return ids * most + jnp.sum(rank * onehot, axis=1)


def place_rows(rows, slot, total):
    return jnp.zeros((total, rows.shape[1]), rows.dtype).at[slot].set(rows)


def shards(source_rows, rel_ids, relations, entities, pos_slot, negatives):
    src_rows, width = source_rows.shape
    rel_dev = relations.shape[0]
    owners = lax.axis_size("rel")
    nrel = rel_dev * owners
    most = 2 * src_rows // nrel
    slot = slot_index(rel_ids, nrel, most)
    sent = place_rows(source_rows, slot, nrel * most).reshape(nrel, most, width)
    every_matrix = gather_relations(relations)
    q_slots = jnp.einsum(
        "kmd,kde->kme", sent, every_matrix, preferred_element_type=jnp.float32
    ).astype(jnp.bfloat16)
    queries = q_slots.reshape(nrel * most, width)[slot]
    state, query_grad = run_stops(
        queries, jnp.transpose(negatives, (0, 2, 1)), pos_slot.reshape(1, -1), entities
    )
    gq_slots = place_rows(query_grad, slot, nrel * most).reshape(nrel, most, width)
    back_slots = jnp.einsum(
        "kme,kde->kmd", gq_slots, every_matrix, preferred_element_type=jnp.float32
    ).astype(jnp.bfloat16)
    by_parity = lambda t: jnp.moveaxis(t.reshape(owners, rel_dev, most, width), 1, 0).reshape(nrel, most, width)
    terms = jnp.einsum(
        "kmd,kme->kde", by_parity(sent), by_parity(gq_slots), preferred_element_type=jnp.float32
    ).astype(jnp.bfloat16)
    source_grad = back_slots.reshape(nrel * most, width)[slot]
    relation_grad = scatter_terms(terms)
    return (state, source_grad, relation_grad)


def solution(mesh):
    placed = (
        P(("cand", "rel"), None),
        P(("cand", "rel"), None),
        P("rel", None, None),
        P(("cand", "rel"), None),
        P(("cand", "rel")),
        P(None, ("cand", "rel"), None),
    )
    return jax.shard_map(
        shards,
        mesh=mesh,
        in_specs=placed,
        out_specs=(P(("cand", "rel"), None), P(("cand", "rel"), None), P("cand", "rel", None)),
        check_vma=False,
    )
```

time: 544 us -> 243 us (0.45); the launches traced: 535 us -> 242 us
  waiting for transfers between devices: 347 us -> 0 us
  Pallas kernels: 0 us -> 151 us
  matrix products: 98.3 us -> 23.5 us
  other arithmetic: 27.7 us -> 7.01 us
  local copies, waits for them, and re-layouts: 43.7 us -> 59.9 us
  between operations: 16.2 us -> 0.71 us
    pallas_call x0 -> x3, Pallas kernels: none -> 151 us  [the longest x1 59.6 us: run_stops(): pl.pallas_call(stops_kernel, out_shape=(jax.ShapeDtypeStruct((part, width...]
    reduce_scatter x1 -> x0, waiting for transfers between devices: 108 us -> none  [shards(): lax.psum_scatter(terms.astype(jnp.bfloat16), 'rel', scatter_dimension=1,...]
    unnamed x4 -> x0, waiting for transfers between devices: 95 us -> none
    all_gather x1 -> x0, waiting for transfers between devices: 88.9 us -> none  [shards(): every_matrix = lax.all_gather(relations, 'rel', axis=0, tiled=True)]
    dot_general x25 -> x1, matrix products: 80 us -> 5.6 us  [shards(): jnp.einsum('kmd,kme->kde', by_parity(sent), by_parity(gq_slots), preferre...]
    ppermute x7 -> x0, waiting for transfers between devices: 55.3 us -> none  [from_behind(): return lax.ppermute(block, axis, route)]
    scatter x1 -> x0, other arithmetic: 17.9 us -> none  [place_rows(): return jnp.zeros((total, rows.shape[1]), rows.dtype).at[slot].set(rows)]
    scatter x1 -> x2, local copies, waits for them, and re-layouts: 12.6 us -> 25.2 us  [place_rows(): return jnp.zeros((total, rows.shape[1]), rows.dtype).at[slot].set(rows)]
  transfers between devices with their start and end apart: 10 -> 0, of which waited for: 10 -> 0; matrix products, arithmetic and copies ran while one was open for 13% -> 0% of each run, Pallas kernels for 0% -> 0%
where the time goes in v1:
time: 243 us; the launch traced here: 242 us
  Pallas kernels  151 us (62%)
  local copies, waits for them, and re-layouts  59.9 us (25%)
  matrix products  23.5 us (10%)
  other arithmetic  7.01 us (3%)
    pallas_call x1, Pallas kernels, run_stops(): pl.pallas_call(stops_kernel, out_shape=(jax.ShapeDtypeStruct((part, width...  59.6 us
    pallas_call x1, Pallas kernels, scatter_terms(): pl.pallas_call(scatter_kernel, out_shape=jax.ShapeDtypeStruct((rows, 2, w...  50.1 us
    pallas_call x1, Pallas kernels, gather_relations(): pl.pallas_call(gather_kernel, out_shape=jax.ShapeDtypeStruct((owners, per...  41.4 us
    scatter x2, local copies, waits for them, and re-layouts, place_rows(): return jnp.zeros((total, rows.shape[1]), rows.dtype).at[slot].set(rows)  25.2 us
    gather x1, local copies, waits for them, and re-layouts, shards(): queries = q_slots.reshape(nrel * most, width)[slot]  12 us
    gather x1, local copies, waits for them, and re-layouts, shards(): source_grad = back_slots.reshape(nrel * most, width)[slot]  12 us
    dot_general x1, matrix products, shards(): jnp.einsum('kme,kde->kmd', gq_slots, every_matrix, preferred_element_type...  8.96 us
    dot_general x1, matrix products, shards(): jnp.einsum('kmd,kde->kme', sent, every_matrix, preferred_element_type=jnp...  8.93 us

profile of v1, /device:TPU:0, one launch (start us, length us, event | category | flops | bytes accessed | tf_op | source)
XLA Modules:
  0.0 242.3 jit_solution(13875043432627556472)
XLA Ops:
  0.6 0.7 fusion.7
  1.3 4.5 %reduce-window.6 = s32[16,16,128]{2,1,0:T(8,128)S(1)} reduce-window(s32[16,16,128]{2,1,0:T(8,128)S(1)} %fusion.7, s32[]{:T(128)} %constant.3.clone.1), window={size=1x1x128 pad=0_0x0_0x127_0}, to_apply=%region_0.0 | reduce-window | flops 4161536 | bytes 262148 | tf_op jit(solution)/shard_map/reduce-window
  5.9 0.4 slice_reduce_fusion
  6.3 0.2 reduce-window.9
  6.5 0.1 broadcast_add_fusion
  6.6 0.8 fusion.6
  7.4 0.7 compare_select_fusion
  8.1 12.6 %scatter_custom_fusion = bf16[4096,512]{1,0:T(8,128)(2,1)} fusion(s32[2048]{0:T(1024)S(1)} %bitcast.63, bf16[2048,512]{1,0:T(8,128)(2,1)} %param.6, bf16[]{:T(256)} %constant.4.clone.1), kind=kCustom, calls=%fused_computation.9 | custom fusion | bytes 4194816 | tf_op jit(solution)/shard_map/scatter | solution.py:454
  20.7 4.5 %copy.9 = bf16[2,8,256,512]{3,2,1,0:T(8,128)(2,1)} copy(bf16[2,8,256,512]{3,2,0,1:T(8,128)(2,1)} %bitcast.50) | data formatting | bytes 8388608 | tf_op jit(solution)/shard_map/transpose | solution.py:477
  25.2 41.4 %gather_relations.1 = bf16[8,2,512,512]{3,2,1,0:T(8,128)(2,1)} custom-call(bf16[2,512,512]{2,1,0:T(8,128)(2,1)} %own.1), custom_call_target="tpu_custom_call" | custom-call | tf_op jit(solution)/shard_map/gather_relations/pallas_call | solution.py:124
  66.7 8.9 %convolution_convert_fusion.2 = bf16[16,256,512]{2,1,0:T(8,128)(2,1)} fusion(bf16[16,256,512]{2,1,0:T(8,128)(2,1)} %bitcast.51, bf16[16,512,512]{2,1,0:T(8,128)(2,1)} %bitcast.47), kind=kOutput, calls=%fused_computation.6 | convolution fusion | flops 2149580800 | bytes 16777216 | tf_op jit(solution)/shard_map/kmd,kde->kme/dot_general | solution.py:466
  75.6 12.0 %gather_fusion = bf16[2048,512]{1,0:T(8,128)(2,1)} fusion(bf16[4096,512]{1,0:T(8,128)(2,1)} %bitcast.46, s32[2048]{0:T(1024)S(1)} %broadcast_clamp_fusion), kind=kCustom, calls=%fused_computation | custom fusion | bytes 4202496 | tf_op jit(solution)/shard_map/gather | solution.py:469
  87.6 59.6 %run_stops.1 = (f32[256,512]{1,0:T(8,128)}, bf16[2048,512]{1,0:T(8,128)(2,1)}) custom-call(bf16[2048,512]{1,0:T(8,128)(2,1)} %gather_fusion, s32[8,16,2048]{2,1,0:T(8,128)} %bitcast.57, s32[1,2048]{1,0:T(1,128)} %bitcast.66, f32[256,512]{1,0:T(8,128)} %entities.1), custom_call_target="tpu_custom_call" | custom-call | tf_op jit(solution)/shard_map/run_stops/pallas_call | solution.py:418
  147.3 12.6 %scatter_custom_fusion.1 = bf16[4096,512]{1,0:T(8,128)(2,1)} fusion(s32[2048]{0:T(1024)S(1)} %bitcast.64, bf16[2048,512]{1,0:T(8,128)(2,1)} %get-tuple-element.6, bf16[]{:T(256)} %constant.4.clone.1), kind=kCustom, calls=%fused_computation.7 | custom fusion | bytes 4194816 | tf_op jit(solution)/shard_map/scatter | solution.py:454
  159.9 9.0 %convolution_convert_fusion.1 = bf16[16,256,512]{2,1,0:T(8,128)(2,1)} fusion(bf16[16,256,512]{2,1,0:T(8,128)(2,1)} %bitcast.52, bf16[16,512,512]{2,1,0:T(8,128)(2,1)} %bitcast.48), kind=kOutput, calls=%fused_computation.5 | convolution fusion | flops 2149580800 | bytes 16777216 | tf_op jit(solution)/shard_map/kme,kde->kmd/dot_general | solution.py:474
  168.8 12.0 %gather_fusion.1 = bf16[2048,512]{1,0:T(8,128)(2,1)} fusion(bf16[4096,512]{1,0:T(8,128)(2,1)} %bitcast.49, s32[2048]{0:T(1024)S(1)} %broadcast_clamp_fusion), kind=kCustom, calls=%fused_computation.1 | custom fusion | bytes 4202496 | tf_op jit(solution)/shard_map/gather | solution.py:481
  180.8 0.0 copy-start
  180.8 2.6 %copy.10 = bf16[2,8,256,512]{3,2,1,0:T(8,128)(2,1)S(1)} copy(bf16[2,8,256,512]{3,2,0,1:T(8,128)(2,1)} %bitcast.53) | data formatting | bytes 8388608 | tf_op jit(solution)/shard_map/transpose | solution.py:477
  183.4 0.8 copy-done
  184.2 5.6 %convolution_convert_fusion = bf16[16,512,512]{2,1,0:T(8,128)(2,1)} fusion(bf16[16,256,512]{2,1,0:T(8,128)(2,1)S(1)} %bitcast.55, bf16[16,256,512]{2,1,0:T(8,128)(2,1)S(1)} %bitcast.56), kind=kOutput, calls=%fused_computation.4 | convolution fusion | flops 2151677952 | bytes 16777216 | tf_op jit(solution)/shard_map/kmd,kme->kde/dot_general | solution.py:478
  189.9 0.0 copy-start.1
  189.9 50.1 %scatter_terms.1 = f32[32,2,512]{2,1,0:T(2,128)} custom-call(bf16[2,2,4,2,4,2,32,512]{7,6,5,4,3,2,1,0:T(8,128)(2,1)} %bitcast.54), custom_call_target="tpu_custom_call" | custom-call | tf_op jit(solution)/shard_map/scatter_terms/pallas_call | solution.py:250
  239.9 0.0 copy-done.1
  240.0 0.8 copy.17
  240.8 1.6 copy.18
  (1 shorter events, 0.0 us)
Async XLA Ops:
  180.8 3.4 %copy-start = (bf16[2,8,256,512]{3,2,1,0:T(8,128)(2,1)S(1)}, bf16[2,8,256,512]{3,2,1,0:T(8,128)(2,1)}, u32[]{:S(2)}) copy-start(bf16[2,8,256,512]{3,2,1,0:T(8,128)(2,1)} %copy.9) | copy-start | bytes 12582916
  189.9 50.1 %copy-start.1 = (f32[256,512]{1,0:T(8,128)S(1)}, f32[256,512]{1,0:T(8,128)}, u32[]{:S(2)}) copy-start(f32[256,512]{1,0:T(8,128)} %get-tuple-element.10) | copy-start | bytes 1572868

commit v2 on v1

--- a/solution.py
+++ b/solution.py
@@ -66,7 +66,147 @@
             copy.wait_send()
 
 
-def gather_kernel(own, out, local_sem, send_sem, recv_sem):
+WINDOW_PAD = 16
+
+
+def sort_plan(ids, nrel):
+    rows = ids.shape[1]
+    block = 256
+    named = (jnp.broadcast_to(ids, (nrel, rows)) == lax.broadcasted_iota(jnp.int32, (nrel, rows), 0)).astype(F32)
+    before = (
+        lax.broadcasted_iota(jnp.int32, (block, block), 0) < lax.broadcasted_iota(jnp.int32, (block, block), 1)
+    ).astype(BF)
+    running = jnp.zeros((nrel, 1), F32)
+    ranks = []
+    for b in range(rows // block):
+        part = named[:, b * block : (b + 1) * block]
+        ranks.append(jnp.dot(part.astype(BF), before, preferred_element_type=F32) + running)
+        running = running + jnp.sum(part, axis=1, keepdims=True)
+    rank = jnp.concatenate(ranks, axis=1)
+    lower = (
+        lax.broadcasted_iota(jnp.int32, (nrel, nrel), 1) < lax.broadcasted_iota(jnp.int32, (nrel, nrel), 0)
+    ).astype(BF)
+    starts = jnp.dot(lower, jnp.broadcast_to(running, (nrel, 128)).astype(BF), preferred_element_type=F32)
+    place = jnp.sum(named * (rank + starts[:, 0:1]), axis=0, keepdims=True)
+    return place, starts
+
+
+def sort_rows(b, place, rows_ref, meta_ref, rows_out, picks_out, pos_out, part):
+    rows = place.shape[1]
+    block = 256
+    here = pl.ds(b * block, block)
+    spot = lax.broadcasted_iota(jnp.int32, (block, rows), 0) + b * block
+    choose = (jnp.broadcast_to(place, (block, rows)) == spot).astype(F32).astype(BF)
+    rows_out[here, :] = jnp.dot(choose, rows_ref[...], preferred_element_type=F32).astype(BF)
+    meta = lax.dot_general(
+        meta_ref[...], choose, (((1,), (1,)), ((), ())), preferred_element_type=F32
+    ).astype(jnp.int32)
+    named = picks_out.shape[0]
+    picks_out[:, here] = meta[0:named]
+    pos_out[:, here] = meta[named : named + 1] * part + meta[named + 1 : named + 2]
+
+
+def group_queries(starts, rows_ref, matrix, out):
+    k = pl.program_id(0)
+    window = out_window(starts, k)
+    rows = rows_ref[window[0], :]
+    new = jnp.dot(rows, matrix[0], preferred_element_type=F32).astype(BF)
+    out[window[0], :] = jnp.where(window[1], new, out[window[0], :])
+
+
+def out_window(starts, k):
+    size = 256 + WINDOW_PAD
+    start, end = starts[k], starts[k + 1]
+    base = pl.multiple_of(start // WINDOW_PAD * WINDOW_PAD, WINDOW_PAD)
+    row = lax.broadcasted_iota(jnp.int32, (size, 512), 0) + base
+    return pl.ds(base, size), (row >= start) & (row < end)
+
+
+def make_queries(starts, rows, matrices):
+    nrel, width, _ = matrices.shape
+    return pl.pallas_call(
+        group_queries,
+        out_shape=jax.ShapeDtypeStruct(rows.shape, BF),
+        grid_spec=pltpu.PrefetchScalarGridSpec(
+            num_scalar_prefetch=1,
+            grid=(nrel,),
+            in_specs=[
+                pl.BlockSpec(rows.shape, lambda k, s: (0, 0)),
+                pl.BlockSpec((1, width, width), lambda k, s: (k, 0, 0)),
+            ],
+            out_specs=pl.BlockSpec(rows.shape, lambda k, s: (0, 0)),
+        ),
+        compiler_params=pltpu.CompilerParams(vmem_limit_bytes=40 << 20),
+        name="make_queries",
+    )(starts, rows, matrices)
+
+
+def group_grads(starts, place, rows_ref, grads, matrix, terms, source_grad, back):
+    step = pl.program_id(0)
+    nrel = 16
+
+    @pl.when(step < nrel)
+    def _():
+        window, inside = out_window(starts, step)
+        grad = grads[window, :]
+        new = lax.dot_general(grad, matrix[0], (((1,), (1,)), ((), ())), preferred_element_type=F32).astype(BF)
+        back[window, :] = jnp.where(inside, new, back[window, :])
+        rows = rows_ref[window, :]
+        rows = jnp.where(inside, rows, jnp.zeros_like(rows))
+        terms[0, 0] = lax.dot_general(
+            rows, grad, (((0,), (0,)), ((), ())), preferred_element_type=F32
+        ).astype(BF)
+
+    @pl.when(step >= nrel)
+    def _():
+        lanes = 128
+        b = step - nrel
+        here = pl.ds(pl.multiple_of(b * lanes, lanes), lanes)
+        mine = jnp.broadcast_to(place[:, here], (lanes, lanes)).T
+        index = lax.broadcasted_iota(jnp.int32, (lanes, lanes), 1)
+        total = place.shape[1]
+        choose = jnp.concatenate(
+            [(mine == index + t * lanes).astype(F32).astype(BF) for t in range(total // lanes)], axis=1
+        )
+        source_grad[...] = jnp.dot(choose, back[0:total, :], preferred_element_type=F32).astype(BF)
+
+
+def make_grads(starts, place, rows, grads, matrices):
+    nrel, width, _ = matrices.shape
+    total = place.shape[1]
+    blocks = total // 128
+    last = lambda k: jnp.minimum(k, nrel - 1)
+    whole = lambda a: pl.BlockSpec(a.shape, lambda k, s: (0, 0))
+    return pl.pallas_call(
+        group_grads,
+        out_shape=(
+            jax.ShapeDtypeStruct((2, nrel // 2, width, width), BF),
+            jax.ShapeDtypeStruct((total, width), BF),
+        ),
+        grid_spec=pltpu.PrefetchScalarGridSpec(
+            num_scalar_prefetch=1,
+            grid=(nrel + blocks,),
+            in_specs=[
+                whole(place),
+                whole(rows),
+                whole(grads),
+                pl.BlockSpec((1, width, width), lambda k, s: (last(k), 0, 0)),
+            ],
+            out_specs=(
+                pl.BlockSpec((1, 1, width, width), lambda k, s: (lax.rem(last(k), 2), last(k) // 2, 0, 0)),
+                pl.BlockSpec((128, width), lambda k, s: (jnp.maximum(k - nrel, 0), 0)),
+            ),
+            scratch_shapes=[pltpu.VMEM(rows.shape, BF)],
+        ),
+        compiler_params=pltpu.CompilerParams(vmem_limit_bytes=40 << 20),
+        name="make_grads",
+    )(starts, place, rows, grads, matrices)
+
+
+def gather_kernel(
+    own, ids, rows_ref, picks, target, out, rows_out, picks_out, target_out, place_out, starts_out, meta,
+    local_sem, send_sem, recv_sem,
+):
     at = Spot()
     mail = Mail(send_sem, recv_sem)
     left, right = at.device(x=turn(at.x, 3)), at.device(x=turn(at.x, 1))
@@ -90,21 +230,47 @@
     to_across = mail.send(own_mine, block(me, x0, mine), across)
     to_right = mail.send(own_mine, block(me, x0, mine), right)
     to_left = mail.send(own_mine, block(me, x0, mine), left)
+
+    stops, samples, total = picks.shape
+    part = total // stops
+    nrel = starts_out.shape[0]
+    place, starts = sort_plan(ids[...], nrel)
+    place = place.astype(jnp.int32)
+    place_out[...] = place
+    starts_out[...] = starts.astype(jnp.int32)
+    for s in range(stops):
+        meta[s * samples : (s + 1) * samples, :] = picks[s].astype(F32).astype(BF)
+    goal = target[...]
+    tail = lax.broadcasted_iota(jnp.int32, (16, total), 0)
+    meta[stops * samples :, :] = jnp.where(
+        tail == 0, jnp.broadcast_to(goal // part, (16, total)), jnp.broadcast_to(lax.rem(goal, part), (16, total))
+    ).astype(F32).astype(BF)
+    rows_out[total:, :] = jnp.zeros((rows_out.shape[0] - total, rows_out.shape[1]), BF)
+
+    def work(b):
+        sort_rows(b, place_out[...], rows_ref, meta, rows_out, picks_out, target_out, part)
+
+    work(0)
     to_right.wait_recv()
     on_right = mail.send(block(me, x3, first), block(me, x3, first), right)
     share = [mail.send(block(me, x3, mine), block(me, x3, mine), partner)]
     to_left.wait_recv()
     on_left = mail.send(block(me, x1, second), block(me, x1, second), left)
     share.append(mail.send(block(me, x1, mine), block(me, x1, mine), partner))
+    work(1)
     to_across.wait_recv()
     far_right = mail.send(block(far, x0, mine), block(far, x0, mine), right)
     far_left = mail.send(block(far, x0, mine), block(far, x0, mine), left)
     share.append(mail.send(block(far, x0, mine), block(far, x0, mine), partner))
+    work(2)
+    work(3)
     on_right.wait_recv()
     opposite_a = mail.send(block(me, x2, first), block(me, x2, first), across)
     on_left.wait_recv()
     opposite_b = mail.send(block(me, x2, second), block(me, x2, second), across)
     share.append(mail.send(block(me, x2, mine), block(me, x2, mine), partner))
+    for b in range(4, 8):
+        work(b)
     far_right.wait_recv()
     share.append(mail.send(block(far, x3, mine), block(far, x3, mine), partner))
     far_left.wait_recv()
@@ -118,152 +284,39 @@
     here.wait()
 
 
-def gather_relations(relations):
+def gather_relations(relations, ids, rows, picks, target):
     per, width, _ = relations.shape
     owners = lax.axis_size("rel")
+    nrel = owners * per
+    stops, samples, total = picks.shape
+    vmem = pl.BlockSpec(memory_space=pltpu.VMEM)
     out = pl.pallas_call(
         gather_kernel,
-        out_shape=jax.ShapeDtypeStruct((owners, per, width, width), relations.dtype),
-        in_specs=[pl.BlockSpec(memory_space=pltpu.VMEM)],
-        out_specs=pl.BlockSpec(memory_space=pl.ANY),
+        out_shape=(
+            jax.ShapeDtypeStruct((owners, per, width, width), relations.dtype),
+            jax.ShapeDtypeStruct((total + 256 + WINDOW_PAD, width), BF),
+            jax.ShapeDtypeStruct((stops * samples, total), jnp.int32),
+            jax.ShapeDtypeStruct((1, total), jnp.int32),
+            jax.ShapeDtypeStruct((1, total), jnp.int32),
+            jax.ShapeDtypeStruct((nrel, 128), jnp.int32),
+        ),
+        in_specs=[vmem] * 5,
+        out_specs=(pl.BlockSpec(memory_space=pl.ANY), *[vmem] * 5),
         scratch_shapes=[
+            pltpu.VMEM((stops * samples + 16, total), BF),
             pltpu.SemaphoreType.DMA,
             pltpu.SemaphoreType.DMA((20,)),
             pltpu.SemaphoreType.DMA((20,)),
         ],
-        compiler_params=pltpu.CompilerParams(collective_id=0, has_side_effects=True),
+        compiler_params=pltpu.CompilerParams(
+            collective_id=0, has_side_effects=True, vmem_limit_bytes=40 << 20
+        ),
         name="gather_relations",
-    )(relations)
-    return out.reshape(owners * per, width, width)
-
-
-def add_into(dst, *others):
-    lead = dst.shape[:-2]
-    total = 1
-    for n in lead:
-        total *= n
-
-    def body(i, carry):
-        index, rest = [], i
-        for n in reversed(lead):
-            index.insert(0, lax.rem(rest, n))
-            rest = rest // n
-        value = dst[tuple(index)].astype(F32)
-        for other in others:
-            value = value + other[tuple(index)].astype(F32)
-        dst[tuple(index)] = value.astype(dst.dtype)
-        return carry
-
-    lax.fori_loop(0, total, body, 0)
-
-
-class Ring:
-    def __init__(self, mail, place, ahead, behind, piece, halves, land_half, land_full):
-        self.mail, self.place, self.ahead, self.behind = mail, place, ahead, behind
-        self.piece, self.halves, self.land_half, self.land_full = piece, halves, land_half, land_full
-
-    def one(self):
-        far = turn(self.place, 2)
-        self.h = [
-            self.mail.send(self.halves(self.piece(far))[d], self.land_half[d], device)
-            for d, device in enumerate((self.ahead, self.behind))
-        ]
-
-    def two(self):
-        self.f = []
-        for d, (step, device) in enumerate(((1, self.ahead), (3, self.behind))):
-            self.h[d].wait_recv()
-            target = self.piece(turn(self.place, step))
-            add_into(self.halves(target)[d], self.land_half[d])
-            self.f.append(self.mail.send(target, self.land_full[d], device))
-
-    def three(self):
-        for copy in self.f:
-            copy.wait_recv()
-        return self.piece(self.place), self.land_full
-
-
-def scatter_kernel(
-    terms, out, got, ax_h, ax_f, ay_h, ay_f, az_h, az_f, by_h, by_f, bx_h, bx_f, bz_h, bz_f, send_sem, recv_sem
-):
-    at = Spot()
-    mail = Mail(send_sem, recv_sem)
-    partner = at.device(core=1 - at.core)
-    xs = at.device(x=turn(at.x, 1)), at.device(x=turn(at.x, 3))
-    ys = at.device(y=turn(at.y, 1)), at.device(y=turn(at.y, 3))
-    zs = at.device(z=turn(at.z, 1)), at.device(z=turn(at.z, 3))
-    greet([partner, *xs, *ys, *zs])
-
-    swap = [mail.send(terms.at[j, :, :, :, :, 1 - at.core], got.at[j], partner) for j in range(2)]
-
-    def first_half(ref):
-        return ref.at[0], ref.at[1]
-
-    def row_halves(ref):
-        rows = ref.shape[0] // 2
-        return ref.at[pl.ds(0, rows)], ref.at[pl.ds(rows, rows)]
-
-    def two(ref):
-        return ref.at[0], ref.at[1]
-
-    a, b = got.at[0], got.at[1]
-    ax = Ring(mail, at.x, *xs, lambda t: a.at[:, t], first_half, two(ax_h), two(ax_f))
-    a1 = lambda: a.at[:, at.x]
-    ay = Ring(mail, at.y, *ys, lambda t: a1().at[:, :, t], first_half, two(ay_h), two(ay_f))
-    a2 = lambda z: a.at[z // 2, at.x, lax.rem(z, 2), at.y]
-    az = Ring(mail, at.z, *zs, a2, row_halves, two(az_h), two(az_f))
-    by = Ring(mail, at.y, *ys, lambda t: b.at[:, :, :, t], first_half, two(by_h), two(by_f))
-    bx = Ring(mail, at.x, *xs, lambda t: b.at[:, t, :, at.y], first_half, two(bx_h), two(bx_f))
-    b2 = lambda z: b.at[z // 2, at.x, lax.rem(z, 2), at.y]
-    bz = Ring(mail, at.z, *zs, b2, row_halves, two(bz_h), two(bz_f))
-
-    for j, (ref, ring) in enumerate(((a, ax), (b, by))):
-        swap[j].wait_recv()
-        add_into(ref, terms.at[j, :, :, :, :, at.core])
-        ring.one()
-    ax.two()
-    by.two()
-    for ring, following in ((ax, ay), (by, bx)):
-        piece, landed = ring.three()
-        add_into(piece, *landed)
-        following.one()
-    ay.two()
-    bx.two()
-    for ring, following in ((ay, az), (bx, bz)):
-        piece, landed = ring.three()
-        add_into(piece, *landed)
-        following.one()
-    az.two()
-    bz.two()
-    for j, ring in enumerate((az, bz)):
-        piece, landed = ring.three()
-        out[:, j, :] = piece[...].astype(F32) + landed[0][...].astype(F32) + landed[1][...].astype(F32)
-    mail.drain()
-
-
-def scatter_terms(terms):
-    nrel, width, _ = terms.shape
-    rows = width // 16
-    shaped = terms.reshape(2, 2, 4, 2, 4, 2, rows, width)
-    v = lambda *lead: pltpu.VMEM((*lead, rows, width), BF)
-    z = lambda r: pltpu.VMEM((2, r, width), BF)
-    return pl.pallas_call(
-        scatter_kernel,
-        out_shape=jax.ShapeDtypeStruct((rows, 2, width), F32),
-        in_specs=[pl.BlockSpec(memory_space=pltpu.VMEM)],
-        out_specs=pl.BlockSpec(memory_space=pltpu.VMEM),
-        scratch_shapes=[
-            v(2, 2, 4, 2, 4),
-            v(2, 2, 4), v(2, 2, 2, 4), v(2, 2), v(2, 2, 2), z(rows // 2), v(2),
-            v(2, 4, 2), v(2, 2, 4, 2), v(2, 2), v(2, 2, 2), z(rows // 2), v(2),
-            pltpu.SemaphoreType.DMA((26,)),
-            pltpu.SemaphoreType.DMA((26,)),
-        ],
-        compiler_params=pltpu.CompilerParams(
-            collective_id=1, has_side_effects=True, vmem_limit_bytes=60 << 20
-        ),
-        name="scatter_terms",
-    )(shaped)
+    )(relations, ids, rows, picks, target)
+    matrices, rows, picks, target, place, starts = out
+    starts = jnp.concatenate([starts[:, 0], jnp.full((1,), total, jnp.int32)])
+    return matrices.reshape(nrel, width, width), rows, picks.reshape(stops, samples, total), target, place, starts
+
 
 STOPS = 8
 learn_rate = 0.005
@@ -279,7 +332,7 @@
     ahead, behind = (lax.rem(cand + 1, n), rel), (lax.rem(cand + n - 1, n), rel)
     greet([ahead, behind])
     part, width = entities.shape
-    rows = q.shape[0]
+    rows = pos.shape[1]
     chunk = part // 2
     parts = part // LOW
     block = 256
@@ -367,7 +420,7 @@
             pieces.append(jnp.where(marks >= 32, up - down, up).astype(BF))
         weight = jnp.concatenate(pieces, axis=1)
         weights[pl.ds(pl.multiple_of(base, chunk), chunk), :] = weight
-        change = jnp.dot(weight, q[...], preferred_element_type=F32)
+        change = jnp.dot(weight, q[0:rows, :], preferred_element_type=F32)
         sent[t] = state - learn_rate * change
 
         @pl.when(t < 2 * STOPS - 2)
@@ -402,6 +455,8 @@
 
     lax.fori_loop(0, rows // block, turned, 0)
 
+    grad_out[rows:, :] = jnp.zeros((grad_out.shape[0] - rows, width), BF)
+
     def drained(t, carry):
         hop(t).wait_send()
         return carry
@@ -410,7 +465,8 @@
 
 
 def run_stops(queries, picks, pos, entities):
-    rows, width = queries.shape
+    padded, width = queries.shape
+    rows = pos.shape[1]
     part = entities.shape[0]
     chunk = part // 2
     vmem = pl.BlockSpec(memory_space=pltpu.VMEM)
@@ -419,7 +475,7 @@
         stops_kernel,
         out_shape=(
             jax.ShapeDtypeStruct((part, width), F32),
-            jax.ShapeDtypeStruct((rows, width), BF),
+            jax.ShapeDtypeStruct((padded, width), BF),
         ),
         in_specs=[vmem, vmem, vmem, pl.BlockSpec(memory_space=pl.ANY)],
         out_specs=(vmem, vmem),
@@ -443,42 +499,147 @@
     )(queries, picks, pos, entities)
 
 
-def slot_index(rel_ids, nrel, most):
-    ids = rel_ids[:, 0]
-    onehot = (ids[:, None] == jnp.arange(nrel, dtype=jnp.int32)[None, :]).astype(jnp.int32)
-    rank = jnp.cumsum(onehot, axis=0) - onehot
-    return ids * most + jnp.sum(rank * onehot, axis=1)
-
-
-def place_rows(rows, slot, total):
-    return jnp.zeros((total, rows.shape[1]), rows.dtype).at[slot].set(rows)
+def add_into(dst, *others):
+    lead = dst.shape[:-2]
+    total = 1
+    for n in lead:
+        total *= n
+
+    def body(i, carry):
+        index, rest = [], i
+        for n in reversed(lead):
+            index.insert(0, lax.rem(rest, n))
+            rest = rest // n
+        value = dst[tuple(index)].astype(F32)
+        for other in others:
+            value = value + other[tuple(index)].astype(F32)
+        dst[tuple(index)] = value.astype(dst.dtype)
+        return carry
+
+    lax.fori_loop(0, total, body, 0)
+
+
+class Ring:
+    def __init__(self, mail, place, ahead, behind, piece, halves, land_half, land_full):
+        self.mail, self.place, self.ahead, self.behind = mail, place, ahead, behind
+        self.piece, self.halves, self.land_half, self.land_full = piece, halves, land_half, land_full
+
+    def one(self):
+        far = turn(self.place, 2)
+        self.h = [
+            self.mail.send(self.halves(self.piece(far))[d], self.land_half[d], device)
+            for d, device in enumerate((self.ahead, self.behind))
+        ]
+
+    def two(self):
+        self.f = []
+        for d, (step, device) in enumerate(((1, self.ahead), (3, self.behind))):
+            self.h[d].wait_recv()
+            target = self.piece(turn(self.place, step))
+            add_into(self.halves(target)[d], self.land_half[d])
+            self.f.append(self.mail.send(target, self.land_full[d], device))
+
+    def three(self):
+        for copy in self.f:
+            copy.wait_recv()
+        return self.piece(self.place), self.land_full
+
+
+def scatter_kernel(
+    terms, out, got, ax_h, ax_f, ay_h, ay_f, az_h, az_f, by_h, by_f, bx_h, bx_f, bz_h, bz_f, send_sem, recv_sem
+):
+    at = Spot()
+    mail = Mail(send_sem, recv_sem)
+    partner = at.device(core=1 - at.core)
+    xs = at.device(x=turn(at.x, 1)), at.device(x=turn(at.x, 3))
+    ys = at.device(y=turn(at.y, 1)), at.device(y=turn(at.y, 3))
+    zs = at.device(z=turn(at.z, 1)), at.device(z=turn(at.z, 3))
+    greet([partner, *xs, *ys, *zs])
+
+    swap = [mail.send(terms.at[j, :, :, :, :, 1 - at.core], got.at[j], partner) for j in range(2)]
+
+    def first_half(ref):
+        return ref.at[0], ref.at[1]
+
+    def row_halves(ref):
+        rows = ref.shape[0] // 2
+        return ref.at[pl.ds(0, rows)], ref.at[pl.ds(rows, rows)]
+
+    def two(ref):
+        return ref.at[0], ref.at[1]
+
+    a, b = got.at[0], got.at[1]
+    ax = Ring(mail, at.x, *xs, lambda t: a.at[:, t], first_half, two(ax_h), two(ax_f))
+    a1 = lambda: a.at[:, at.x]
+    ay = Ring(mail, at.y, *ys, lambda t: a1().at[:, :, t], first_half, two(ay_h), two(ay_f))
+    a2 = lambda z: a.at[z // 2, at.x, lax.rem(z, 2), at.y]
+    az = Ring(mail, at.z, *zs, a2, row_halves, two(az_h), two(az_f))
+    by = Ring(mail, at.y, *ys, lambda t: b.at[:, :, :, t], first_half, two(by_h), two(by_f))
+    bx = Ring(mail, at.x, *xs, lambda t: b.at[:, t, :, at.y], first_half, two(bx_h), two(bx_f))
+    b2 = lambda z: b.at[z // 2, at.x, lax.rem(z, 2), at.y]
+    bz = Ring(mail, at.z, *zs, b2, row_halves, two(bz_h), two(bz_f))
+
+    for j, (ref, ring) in enumerate(((a, ax), (b, by))):
+        swap[j].wait_recv()
+        add_into(ref, terms.at[j, :, :, :, :, at.core])
+        ring.one()
+    ax.two()
+    by.two()
+    for ring, following in ((ax, ay), (by, bx)):
+        piece, landed = ring.three()
+        add_into(piece, *landed)
+        following.one()
+    ay.two()
+    bx.two()
+    for ring, following in ((ay, az), (bx, bz)):
+        piece, landed = ring.three()
+        add_into(piece, *landed)
+        following.one()
+    az.two()
+    bz.two()
+    for j, ring in enumerate((az, bz)):
+        piece, landed = ring.three()
+        out[:, j, :] = piece[...].astype(F32) + landed[0][...].astype(F32) + landed[1][...].astype(F32)
+    mail.drain()
+
+
+def scatter_terms(terms):
+    width = terms.shape[-1]
+    rows = width // 16
+    shaped = terms.reshape(2, 2, 4, 2, 4, 2, rows, width)
+    v = lambda *lead: pltpu.VMEM((*lead, rows, width), BF)
+    z = lambda r: pltpu.VMEM((2, r, width), BF)
+    return pl.pallas_call(
+        scatter_kernel,
+        out_shape=jax.ShapeDtypeStruct((rows, 2, width), F32),
+        in_specs=[pl.BlockSpec(memory_space=pltpu.VMEM)],
+        out_specs=pl.BlockSpec(memory_space=pltpu.VMEM),
+        scratch_shapes=[
+            v(2, 2, 4, 2, 4),
+            v(2, 2, 4), v(2, 2, 2, 4), v(2, 2), v(2, 2, 2), z(rows // 2), v(2),
+            v(2, 4, 2), v(2, 2, 4, 2), v(2, 2), v(2, 2, 2), z(rows // 2), v(2),
+            pltpu.SemaphoreType.DMA((26,)),
+            pltpu.SemaphoreType.DMA((26,)),
+        ],
+        compiler_params=pltpu.CompilerParams(
+            collective_id=1, has_side_effects=True, vmem_limit_bytes=60 << 20
+        ),
+        name="scatter_terms",
+    )(shaped)
 
 
 def shards(source_rows, rel_ids, relations, entities, pos_slot, negatives):
-    src_rows, width = source_rows.shape
-    rel_dev = relations.shape[0]
-    owners = lax.axis_size("rel")
-    nrel = rel_dev * owners
-    most = 2 * src_rows // nrel
-    slot = slot_index(rel_ids, nrel, most)
-    sent = place_rows(source_rows, slot, nrel * most).reshape(nrel, most, width)
-    every_matrix = gather_relations(relations)
-    q_slots = jnp.einsum(
-        "kmd,kde->kme", sent, every_matrix, preferred_element_type=jnp.float32
-    ).astype(jnp.bfloat16)
-    queries = q_slots.reshape(nrel * most, width)[slot]
-    state, query_grad = run_stops(
-        queries, jnp.transpose(negatives, (0, 2, 1)), pos_slot.reshape(1, -1), entities
+    rows = source_rows.shape[0]
+    matrices, sorted_rows, picks, target, place, starts = gather_relations(
+        relations,
+        rel_ids.reshape(1, rows),
+        source_rows,
+        jnp.transpose(negatives, (0, 2, 1)),
+        pos_slot.reshape(1, rows),
     )
-    gq_slots = place_rows(query_grad, slot, nrel * most).reshape(nrel, most, width)
-    back_slots = jnp.einsum(
-        "kme,kde->kmd", gq_slots, every_matrix, preferred_element_type=jnp.float32
-    ).astype(jnp.bfloat16)
-    by_parity = lambda t: jnp.moveaxis(t.reshape(owners, rel_dev, most, width), 1, 0).reshape(nrel, most, width)
-    terms = jnp.einsum(
-        "kmd,kme->kde", by_parity(sent), by_parity(gq_slots), preferred_element_type=jnp.float32
-    ).astype(jnp.bfloat16)
-    source_grad = back_slots.reshape(nrel * most, width)[slot]
+    queries = make_queries(starts, sorted_rows, matrices)
+    state, query_grad = run_stops(queries, picks, target, entities)
+    terms, source_grad = make_grads(starts, place, sorted_rows, query_grad, matrices)
     relation_grad = scatter_terms(terms)
     return (state, source_grad, relation_grad)
 

time: 243 us -> 201 us (0.83)
  local copies, waits for them, and re-layouts: 59.9 us -> 19 us
  Pallas kernels: 151 us -> 181 us
  matrix products: 23.5 us -> 0 us
  other arithmetic: 7.01 us -> 0.08 us
    pallas_call x1 -> x3, Pallas kernels: 41.4 us -> 70.7 us  [the longest x1 40.2 us: gather_relations(): pl.pallas_call(gather_kernel, out_shape=(jax.ShapeDtypeStruct((owners, pe...]
    scatter x2 -> x0, local copies, waits for them, and re-layouts: 25.2 us -> none  [place_rows(): return jnp.zeros((total, rows.shape[1]), rows.dtype).at[slot].set(rows)]
    gather x2 -> x0, local copies, waits for them, and re-layouts: 24 us -> none  [the longest x1 12 us: shards(): queries = q_slots.reshape(nrel * most, width)[slot]]
    dot_general x3 -> x0, matrix products: 23.5 us -> none  [the longest x1 8.96 us: shards(): jnp.einsum('kme,kde->kmd', gq_slots, every_matrix, preferred_element_type...]
    unnamed x6 -> x26, local copies, waits for them, and re-layouts: 3.19 us -> 18.9 us
    transpose x2 -> x0, local copies, waits for them, and re-layouts: 7.15 us -> none  [shards(): jnp.moveaxis(t.reshape(owners, rel_dev, most, width), 1, 0)]
    another operation x3 -> x0, other arithmetic: 4.82 us -> none
where the time goes in v2:
time: 201 us; the launch traced here: 200 us
  Pallas kernels  181 us (90%)
  local copies, waits for them, and re-layouts  19 us (9%)
    pallas_call x1, Pallas kernels, run_stops(): pl.pallas_call(stops_kernel, out_shape=(jax.ShapeDtypeStruct((part, width...  59.9 us
    pallas_call x1, Pallas kernels, scatter_terms(): pl.pallas_call(scatter_kernel, out_shape=jax.ShapeDtypeStruct((rows, 2, w...  50.1 us
    pallas_call x1, Pallas kernels, gather_relations(): pl.pallas_call(gather_kernel, out_shape=(jax.ShapeDtypeStruct((owners, pe...  40.2 us
    pallas_call x1, Pallas kernels, make_grads(): pl.pallas_call(group_grads, out_shape=(jax.ShapeDtypeStruct((2, nrel // 2...  24.7 us
    unnamed x26, local copies, waits for them, and re-layouts  18.9 us
    pallas_call x1, Pallas kernels, make_queries(): pl.pallas_call(group_queries, out_shape=jax.ShapeDtypeStruct(rows.shape,...  5.72 us

profile of v2, /device:TPU:0, one launch (start us, length us, event | category | flops | bytes accessed | tf_op | source)
XLA Modules:
  0.0 200.4 jit_solution(12333963192697924670)
XLA Ops:
  0.6 0.0 copy-start.4
  0.6 1.6 copy-done.4
  2.2 0.0 copy-start.5
  2.2 1.2 copy-done.5
  3.4 0.0 copy-start.6
  3.5 1.2 copy-done.6
  4.7 0.0 copy-start.8
  4.7 0.7 copy-done.8
  5.4 0.0 copy-start.9
  5.4 0.7 copy-done.9
  6.1 40.2 %gather_relations.1 = (bf16[8,2,512,512]{3,2,1,0:T(8,128)(2,1)}, bf16[2320,512]{1,0:T(8,128)(2,1)S(1)}, s32[128,2048]{1,0:T(8,128)S(1)}, s32[1,2048]{1,0:T(1,128...) custom-call(bf16[2,512,512]{2,1,0:T(8,128)(2,1)S(1)} %copy-done.5, s32[1,2048]{1,0:T(1,128)S(1)} %bitcast.11, ...), custom_call_target="tpu_custom_call" | custom-call | tf_op jit(solution)/shard_map/gather_relations/pallas_call | solution.py:293
  46.3 0.0 copy-start.7
  46.3 1.0 copy-done.7
  47.3 0.0 copy-start.10
  47.3 0.1 slice_reduce_fusion
  47.4 0.1 pad_add_fusion.starts
  47.5 0.4 copy-done.10
  47.9 0.0 copy-start
  47.9 3.4 %copy-done = bf16[8,2,512,512]{3,2,1,0:T(8,128)(2,1)S(1)} copy-done((bf16[8,2,512,512]{3,2,1,0:T(8,128)(2,1)S(1)}, bf16[8,2,512,512]{3,2,1,0:T(8,128)(2,1)}, u32[]{:S(2)}) %copy-start) | copy-done | bytes 8388632
  51.3 5.7 %make_queries.1.q = bf16[2320,512]{1,0:T(8,128)(2,1)S(1)} custom-call(s32[17]{0:T(128)S(1)} %pad_add_fusion.starts, bf16[2320,512]{1,0:T(8,128)(2,1)S(1)} %get-tuple-element.14.rows_ref, bf16[16,512,512]{2,1,0:T(8,128)(2,1)S(1)} %bitcast.7), custom_call_target="tpu_custom_call" | custom-call | tf_op jit(solution)/shard_map/make_queries/pallas_call | solution.py:127
  57.0 0.0 copy-start.1
  57.0 1.5 copy-done.1
  58.5 59.9 %run_stops.1 = (f32[256,512]{1,0:T(8,128)}, bf16[2320,512]{1,0:T(8,128)(2,1)}) custom-call(bf16[2320,512]{1,0:T(8,128)(2,1)} %copy-done.1, s32[8,16,2048]{2,1,0:T(8,128)} %bitcast.10, s32[1,2048]{1,0:T(1,128)} %copy-done.10, f32[256,512]{1,0:T(8,128)} %entities.1), custom_call_target="tpu_custom_call" | custom-call | tf_op jit(solution)/shard_map/run_stops/pallas_call | solution.py:474
  118.4 0.0 copy-start.3
  118.4 1.7 copy-done.3
  120.1 24.7 %make_grads.1 = (bf16[2,8,512,512]{3,2,1,0:T(8,128)(2,1)S(1)}, bf16[2048,512]{1,0:T(8,128)(2,1)}) custom-call(s32[17]{0:T(128)S(1)} %pad_add_fusion.starts, s32[1,2048]{1,0:T(1,128)S(1)} %get-tuple-element.19.place, bf16[2320,512]{1,0:T(8,128)(2,1)S(1)} %get-tuple-element.14.rows_ref, bf16[2320,512]{1,0:T(8,128)(2,1)S(1)} %copy-done.3, ...), custom_call_target="tpu_custom_call" | custom-call | tf_op jit(solution)/shard_map/make_grads/pallas_call | solution.py:180
  144.7 0.0 copy-start.2
  144.7 3.2 %copy-done.2 = bf16[2,8,512,512]{3,2,1,0:T(8,128)(2,1)} copy-done((bf16[2,8,512,512]{3,2,1,0:T(8,128)(2,1)}, bf16[2,8,512,512]{3,2,1,0:T(8,128)(2,1)S(1)}, u32[]{:S(2)}) %copy-start.2) | copy-done | bytes 8388632
  148.0 50.1 %scatter_terms.1 = f32[32,2,512]{2,1,0:T(2,128)} custom-call(bf16[2,2,4,2,4,2,32,512]{7,6,5,4,3,2,1,0:T(8,128)(2,1)} %bitcast.8), custom_call_target="tpu_custom_call" | custom-call | tf_op jit(solution)/shard_map/scatter_terms/pallas_call | solution.py:612
  198.1 0.0 copy-done.11
  198.1 0.8 copy.11
  198.9 1.6 copy.12
  (1 shorter events, 0.0 us)
Async XLA Ops:
  0.6 1.6 copy-start.4
  2.2 1.2 copy-start.5
  3.4 1.2 copy-start.6
  4.7 0.7 copy-start.8
  5.4 0.7 copy-start.9
  46.3 1.0 copy-start.7
  47.3 0.6 copy-start.10
  47.9 3.4 %copy-start = (bf16[8,2,512,512]{3,2,1,0:T(8,128)(2,1)S(1)}, bf16[8,2,512,512]{3,2,1,0:T(8,128)(2,1)}, u32[]{:S(2)}) copy-start(bf16[8,2,512,512]{3,2,1,0:T(8,128)(2,1)} %get-tuple-element.15) | copy-start | bytes 25165828
  57.0 1.5 copy-start.1
  118.4 1.7 copy-start.3
  144.7 3.2 %copy-start.2 = (bf16[2,8,512,512]{3,2,1,0:T(8,128)(2,1)}, bf16[2,8,512,512]{3,2,1,0:T(8,128)(2,1)S(1)}, u32[]{:S(2)}) copy-start(bf16[2,8,512,512]{3,2,1,0:T(8,128)(2,1)S(1)} %get-tuple-element.22) | copy-start | bytes 25165828
  148.0 50.1 %copy-start.11 = (f32[256,512]{1,0:T(8,128)S(1)}, f32[256,512]{1,0:T(8,128)}, u32[]{:S(2)}) copy-start(f32[256,512]{1,0:T(8,128)} %get-tuple-element.26) | copy-start | bytes 1572868

commit v3 on v2

v3 whole, which is shorter than its diff:
```python
import functools

import jax
import jax.numpy as jnp
from jax import lax
from jax.experimental import pallas as pl
from jax.experimental.pallas import tpu as pltpu
from jax.sharding import PartitionSpec as P

MESH = pl.DeviceIdType.MESH
BF = jnp.bfloat16
F32 = jnp.float32


class Spot:
    def __init__(self):
        cand, rel = lax.axis_index("cand"), lax.axis_index("rel")
        self.core = lax.rem(cand, 2)
        self.y = lax.rem(cand // 2, 4)
        self.zl = cand // 8
        self.x = lax.rem(rel, 4)
        self.zh = rel // 4
        self.z = self.zh * 2 + self.zl
        self.rel = rel

    def device(self, x=None, y=None, z=None, core=None):
        x = self.x if x is None else x
        y = self.y if y is None else y
        z = self.z if z is None else z
        core = self.core if core is None else core
        return ((lax.rem(z, 2) * 4 + y) * 2 + core, (z // 2) * 4 + x)


def turn(i, by):
    return lax.rem(i + by, 4)


def greet(devices):
    barrier = pltpu.get_barrier_semaphore()
    for device in devices:
        pl.semaphore_signal(barrier, inc=1, device_id=device, device_id_type=MESH)
    pl.semaphore_wait(barrier, len(devices))


class Mail:
    def __init__(self, send_sem, recv_sem):
        self.send_sem, self.recv_sem, self.count, self.sent = send_sem, recv_sem, 0, []

    def send(self, src, dst, device):
        i = self.count
        self.count += 1
        copy = pltpu.make_async_remote_copy(
            src_ref=src,
            dst_ref=dst,
            send_sem=self.send_sem.at[i],
            recv_sem=self.recv_sem.at[i],
            device_id=device,
            device_id_type=MESH,
        )
        copy.start()
        self.sent.append(copy)
        return copy

    def drain(self):
        for copy in self.sent:
            copy.wait_send()


WINDOW_PAD = 16


def sort_plan(ids, nrel):
    rows = ids.shape[1]
    block = 256
    named = (jnp.broadcast_to(ids, (nrel, rows)) == lax.broadcasted_iota(jnp.int32, (nrel, rows), 0)).astype(F32)
    before = (
        lax.broadcasted_iota(jnp.int32, (block, block), 0) < lax.broadcasted_iota(jnp.int32, (block, block), 1)
    ).astype(BF)
    running = jnp.zeros((nrel, 1), F32)
    ranks = []
    for b in range(rows // block):
        part = named[:, b * block : (b + 1) * block]
        ranks.append(jnp.dot(part.astype(BF), before, preferred_element_type=F32) + running)
        running = running + jnp.sum(part, axis=1, keepdims=True)
    rank = jnp.concatenate(ranks, axis=1)
    lower = (
        lax.broadcasted_iota(jnp.int32, (nrel, nrel), 1) < lax.broadcasted_iota(jnp.int32, (nrel, nrel), 0)
    ).astype(BF)
    starts = jnp.dot(lower, jnp.broadcast_to(running, (nrel, 128)).astype(BF), preferred_element_type=F32)
    place = jnp.sum(named * (rank + starts[:, 0:1]), axis=0, keepdims=True)
    return place, starts


def sort_rows(b, place, rows_ref, meta_ref, rows_out, picks_out, pos_out, part):
    rows = place.shape[1]
    block = 256
    here = pl.ds(b * block, block)
    spot = lax.broadcasted_iota(jnp.int32, (block, rows), 0) + b * block
    choose = (jnp.broadcast_to(place, (block, rows)) == spot).astype(F32).astype(BF)
    rows_out[here, :] = jnp.dot(choose, rows_ref[...], preferred_element_type=F32).astype(BF)
    meta = lax.dot_general(
        meta_ref[...], choose, (((1,), (1,)), ((), ())), preferred_element_type=F32
    ).astype(jnp.int32)
    named = picks_out.shape[0]
    picks_out[:, here] = meta[0:named]
    pos_out[:, here] = meta[named : named + 1] * part + meta[named + 1 : named + 2]


def group_queries(starts, rows_ref, matrix, out):
    k = pl.program_id(0)
    window = out_window(starts, k)
    rows = rows_ref[window[0], :]
    new = jnp.dot(rows, matrix[0], preferred_element_type=F32).astype(BF)
    out[window[0], :] = jnp.where(window[1], new, out[window[0], :])


def out_window(starts, k):
    size = 256 + WINDOW_PAD
    start, end = starts[k], starts[k + 1]
    base = pl.multiple_of(start // WINDOW_PAD * WINDOW_PAD, WINDOW_PAD)
    row = lax.broadcasted_iota(jnp.int32, (size, 512), 0) + base
    return pl.ds(base, size), (row >= start) & (row < end)


def make_queries(starts, rows, matrices):
    nrel, width, _ = matrices.shape
    return pl.pallas_call(
        group_queries,
        out_shape=jax.ShapeDtypeStruct(rows.shape, BF),
        grid_spec=pltpu.PrefetchScalarGridSpec(
            num_scalar_prefetch=1,
            grid=(nrel,),
            in_specs=[
                pl.BlockSpec(rows.shape, lambda k, s: (0, 0)),
                pl.BlockSpec((1, width, width), lambda k, s: (k, 0, 0)),
            ],
            out_specs=pl.BlockSpec(rows.shape, lambda k, s: (0, 0)),
        ),
        compiler_params=pltpu.CompilerParams(vmem_limit_bytes=20 << 20),
        name="make_queries",
    )(starts, rows, matrices)


def group_grads(starts, rows_ref, grads, matrix, back, terms):
    window, inside = out_window(starts, pl.program_id(0))
    grad = grads[window, :]
    new = lax.dot_general(grad, matrix[0], (((1,), (1,)), ((), ())), preferred_element_type=F32).astype(BF)
    back[window, :] = jnp.where(inside, new, back[window, :])
    rows = rows_ref[window, :]
    rows = jnp.where(inside, rows, jnp.zeros_like(rows))
    terms[0, 0] = lax.dot_general(rows, grad, (((0,), (0,)), ((), ())), preferred_element_type=F32).astype(BF)


def make_grads(starts, rows, grads, matrices):
    nrel, width, _ = matrices.shape
    whole = pl.BlockSpec(grads.shape, lambda k, s: (0, 0))
    return pl.pallas_call(
        group_grads,
        out_shape=(
            jax.ShapeDtypeStruct(grads.shape, BF),
            jax.ShapeDtypeStruct((2, nrel // 2, width, width), BF),
        ),
        grid_spec=pltpu.PrefetchScalarGridSpec(
            num_scalar_prefetch=1,
            grid=(nrel,),
            in_specs=[whole, whole, pl.BlockSpec((1, width, width), lambda k, s: (k, 0, 0))],
            out_specs=(
                whole,
                pl.BlockSpec((1, 1, width, width), lambda k, s: (lax.rem(k, 2), k // 2, 0, 0)),
            ),
        ),
        compiler_params=pltpu.CompilerParams(vmem_limit_bytes=20 << 20),
        name="make_grads",
    )(starts, rows, grads, matrices)


LOW = 64


def tally(stop, part, picks, pos, low, unit, packed):
    samples = 16
    rows = pos.shape[1]
    lanes = 128
    names = picks[pl.ds(pl.multiple_of(stop * samples, samples), samples), :]
    low[0:samples, :] = lax.bitwise_and(names, LOW - 1)
    unit[0:samples, :] = lax.shift_left(jnp.ones_like(names), 8 * lax.shift_right_logical(names, 6))
    place = pos[...] - stop * part
    inside = (place >= 0) & (place < part)
    place = jnp.where(inside, place, 0)
    low[samples : samples + 1, :] = lax.bitwise_and(place, LOW - 1)
    unit[samples : samples + 1, :] = jnp.where(
        inside, lax.shift_left(jnp.full_like(place, 33), 8 * lax.shift_right_logical(place, 6)), 0
    )

    def column(c, carry):
        here = pl.ds(pl.multiple_of(c * lanes, lanes), lanes)
        index = lax.broadcasted_iota(jnp.int32, (LOW, lanes), 0)
        total = jnp.zeros((LOW, lanes), jnp.int32)
        for k in range(samples + 1):
            match = jnp.broadcast_to(low[k : k + 1, here], (LOW, lanes)) == index
            total = total + jnp.where(match, jnp.broadcast_to(unit[k : k + 1, here], (LOW, lanes)), 0)
        packed[stop, :, here] = total
        return carry

    lax.fori_loop(0, rows // lanes, column, 0)


def gather_kernel(
    own, ids, rows_ref, picks, target, out, rows_out, packed, place_out, starts_out,
    meta, sorted_picks, sorted_target, low, unit, local_sem, send_sem, recv_sem,
):
    at = Spot()
    mail = Mail(send_sem, recv_sem)
    left, right = at.device(x=turn(at.x, 3)), at.device(x=turn(at.x, 1))
    down, up = at.device(y=turn(at.y, 3)), at.device(y=turn(at.y, 1))
    across = at.device(z=3 - at.z)
    partner = at.device(core=1 - at.core)
    greet([left, right, down, up, across, partner])
    half = own.shape[1] // 2
    share = half // 4

    def rows(start, size, step):
        return pl.ds(pl.multiple_of(start, step), size)

    start = at.core * half
    mine, first, second = rows(start, half, half), rows(start, half // 2, half), rows(start + half // 2, half // 2, half // 2)

    def quarter(y):
        return rows(start + y * share, share, share)

    def quarter_halves(y):
        return (
            rows(start + y * share, share // 2, share),
            rows(start + y * share + share // 2, share // 2, share // 2),
        )

    me, far = at.zh * 4, (1 - at.zh) * 4
    x0, x1, x2, x3 = at.x, turn(at.x, 1), turn(at.x, 2), turn(at.x, 3)
    y0, y1, y2, y3 = at.y, turn(at.y, 1), turn(at.y, 2), turn(at.y, 3)
    here = [
        pltpu.make_async_copy(own.at[0], out.at[at.rel, 0], local_sem.at[0]),
        pltpu.make_async_copy(own.at[1, quarter(y0)], out.at[at.rel, 1, quarter(y0)], local_sem.at[1]),
    ]
    for copy in here:
        copy.start()

    def same(ref, device):
        return mail.send(ref, ref, device)

    def a(base, x, rows):
        return out.at[base + x, 0, rows]

    def b(base, x, rows):
        return out.at[base + x, 1, rows]

    def b4(base, rows):
        return out.at[pl.ds(base, 4), 1, rows]

    own_a, own_b = own.at[0, mine], own.at[1, quarter(y0)]
    b_across = mail.send(own_b, b(me, x0, quarter(y0)), across)
    b_right = mail.send(own_b, b(me, x0, quarter(y0)), right)
    b_left = mail.send(own_b, b(me, x0, quarter(y0)), left)
    a_across = mail.send(own_a, a(me, x0, mine), across)
    a_right = mail.send(own_a, a(me, x0, mine), right)
    a_left = mail.send(own_a, a(me, x0, mine), left)

    stops, samples, total = picks.shape
    part = total // stops
    nrel = starts_out.shape[0]
    place, starts = sort_plan(ids[...], nrel)
    place = place.astype(jnp.int32)
    place_out[...] = place
    starts_out[...] = starts.astype(jnp.int32)
    for s in range(stops):
        meta[s * samples : (s + 1) * samples, :] = picks[s].astype(F32).astype(BF)
    goal = target[...]
    tail = lax.broadcasted_iota(jnp.int32, (16, total), 0)
    meta[stops * samples :, :] = jnp.where(
        tail == 0, jnp.broadcast_to(goal // part, (16, total)), jnp.broadcast_to(lax.rem(goal, part), (16, total))
    ).astype(F32).astype(BF)
    rows_out[total:, :] = jnp.zeros((rows_out.shape[0] - total, rows_out.shape[1]), BF)

    def work(b):
        sort_rows(b, place_out[...], rows_ref, meta, rows_out, sorted_picks, sorted_target, part)

    def count(s):
        tally(s, part, sorted_picks, sorted_target, low, unit, packed)

    work(0)
    h0, h1 = quarter_halves(y0)
    b_right.wait_recv()
    b_on_right = same(b(me, x3, h0), right)
    b_left.wait_recv()
    b_on_left = same(b(me, x1, h1), left)
    b_across.wait_recv()
    b_far_right = same(b(far, x0, quarter(y0)), right)
    b_far_left = same(b(far, x0, quarter(y0)), left)
    work(1)
    a_right.wait_recv()
    a_on_right = same(a(me, x3, first), right)
    gifts = [same(a(me, x3, mine), partner)]
    a_left.wait_recv()
    a_on_left = same(a(me, x1, second), left)
    gifts.append(same(a(me, x1, mine), partner))
    work(2)
    b_on_right.wait_recv()
    b_on_left.wait_recv()
    here[1].wait()
    me_up, me_down = same(b4(me, quarter(y0)), up), same(b4(me, quarter(y0)), down)
    b_far_right.wait_recv()
    b_far_on_right = same(b(far, x3, h0), right)
    b_far_left.wait_recv()
    b_far_on_left = same(b(far, x1, h1), left)
    work(3)
    a_across.wait_recv()
    a_far_right = same(a(far, x0, mine), right)
    a_far_left = same(a(far, x0, mine), left)
    gifts.append(same(a(far, x0, mine), partner))
    work(4)
    b_far_on_right.wait_recv()
    b_far_on_left.wait_recv()
    far_up, far_down = same(b4(far, quarter(y0)), up), same(b4(far, quarter(y0)), down)
    a_on_right.wait_recv()
    a_opposite = [same(a(me, x2, first), across)]
    a_on_left.wait_recv()
    a_opposite.append(same(a(me, x2, second), across))
    gifts.append(same(a(me, x2, mine), partner))
    work(5)
    me_up.wait_recv()
    me_on_up = same(b4(me, quarter_halves(y3)[0]), up)
    me_down.wait_recv()
    me_on_down = same(b4(me, quarter_halves(y1)[1]), down)
    work(6)
    work(7)
    count(0)
    far_up.wait_recv()
    far_on_up = same(b4(far, quarter_halves(y3)[0]), up)
    far_down.wait_recv()
    far_on_down = same(b4(far, quarter_halves(y1)[1]), down)
    count(1)
    a_far_right.wait_recv()
    gifts.append(same(a(far, x3, mine), partner))
    a_far_left.wait_recv()
    gifts.append(same(a(far, x1, mine), partner))
    count(2)
    me_on_up.wait_recv()
    me_on_down.wait_recv()
    gifts.append(same(b4(me, mine), partner))
    for copy in a_opposite:
        copy.wait_recv()
    gifts.append(same(a(far, x2, mine), partner))
    count(3)
    count(4)
    far_on_up.wait_recv()
    far_on_down.wait_recv()
    gifts.append(same(b4(far, mine), partner))

    def later(s, carry):
        count(s)
        return carry

    lax.fori_loop(5, stops, later, 0)
    for copy in gifts:
        copy.wait_recv()
    mail.drain()
    here[0].wait()


def gather_relations(relations, ids, rows, picks, target):
    per, width, _ = relations.shape
    owners = lax.axis_size("rel")
    nrel = owners * per
    stops, samples, total = picks.shape
    vmem = pl.BlockSpec(memory_space=pltpu.VMEM)
    out = pl.pallas_call(
        gather_kernel,
        out_shape=(
            jax.ShapeDtypeStruct((owners, per, width, width), relations.dtype),
            jax.ShapeDtypeStruct((total + 256 + WINDOW_PAD, width), BF),
            jax.ShapeDtypeStruct((stops, LOW, total), jnp.int32),
            jax.ShapeDtypeStruct((1, total), jnp.int32),
            jax.ShapeDtypeStruct((nrel, 128), jnp.int32),
        ),
        in_specs=[vmem] * 5,
        out_specs=(pl.BlockSpec(memory_space=pl.ANY), *[vmem] * 4),
        scratch_shapes=[
            pltpu.VMEM((stops * samples + 16, total), BF),
            pltpu.VMEM((stops * samples, total), jnp.int32),
            pltpu.VMEM((1, total), jnp.int32),
            pltpu.VMEM((24, total), jnp.int32),
            pltpu.VMEM((24, total), jnp.int32),
            pltpu.SemaphoreType.DMA((2,)),
            pltpu.SemaphoreType.DMA((36,)),
            pltpu.SemaphoreType.DMA((36,)),
        ],
        compiler_params=pltpu.CompilerParams(
            collective_id=0, has_side_effects=True, vmem_limit_bytes=24 << 20
        ),
        name="gather_relations",
    )(relations, ids, rows, picks, target)
    matrices, rows, packed, place, starts = out
    starts = jnp.concatenate([starts[:, 0], jnp.full((1,), total, jnp.int32)])
    return matrices.reshape(nrel, width, width), rows, packed, place, starts


STOPS = 8
learn_rate = 0.005


def stops_kernel(
    q, packed, entities, state_out, grad_out, held, sent, wide, turned_wide, weights, acc, local_sem, send_sem, recv_sem
):
    cand, rel = lax.axis_index("cand"), lax.axis_index("rel")
    n = lax.axis_size("cand")
    ahead, behind = (lax.rem(cand + 1, n), rel), (lax.rem(cand + n - 1, n), rel)
    greet([ahead, behind])
    part, width = entities.shape
    rows = packed.shape[2]
    chunk = part // 2
    block = 256

    fetch = [
        pltpu.make_async_copy(entities.at[pl.ds(h * chunk, chunk)], held.at[h], local_sem.at[h])
        for h in range(2)
    ]
    for copy in fetch:
        copy.start()
    acc[...] = jnp.zeros_like(acc)
    for copy in fetch:
        copy.wait()

    def hop(t):
        return pltpu.make_async_remote_copy(
            src_ref=sent.at[t],
            dst_ref=held.at[t + 2],
            send_sem=send_sem.at[t],
            recv_sem=recv_sem.at[t],
            device_id=ahead,
            device_id_type=MESH,
        )

    def step(t, carry):
        half = lax.rem(t, 2)
        stop = t // 2
        here_rows = pl.ds(pl.multiple_of(half * chunk, chunk), chunk)

        @pl.when(t >= 2)
        def _():
            hop(t - 2).wait_recv()

        state = held[t]
        rounded = state.astype(BF)
        wide[here_rows, :] = rounded
        pieces = []
        for i in range(rows // block):
            here = pl.ds(i * block, block)
            logits = lax.dot_general(
                rounded, q[here, :], (((1,), (1,)), ((), ())), preferred_element_type=F32
            )
            marks = packed[stop, :, here]
            marks = jnp.concatenate(
                [lax.shift_right_logical(marks, 16 * half + 8 * p) for p in range(chunk // LOW)], axis=0
            )
            named = lax.bitwise_and(marks, 31).astype(F32)
            chance = 1.0 / (1.0 + jnp.exp(-logits))
            product = named * chance
            pieces.append(jnp.where(lax.bitwise_and(marks, 32) != 0, product - 1.0, product).astype(BF))
        weight = jnp.concatenate(pieces, axis=1)
        weights[here_rows, :] = weight
        change = jnp.dot(weight, q[0:rows, :], preferred_element_type=F32)
        sent[t] = state - learn_rate * change

        @pl.when(t < 2 * STOPS - 2)
        def _():
            hop(t).start()

        @pl.when(half == 1)
        def _():
            turned_wide[...] = wide[...].astype(F32).T.astype(BF)
            big = 512

            def gather(c, carry):
                here = pl.ds(pl.multiple_of(c * big, big), big)
                acc[:, here] += jnp.dot(turned_wide[...], weights[:, here], preferred_element_type=F32)
                return carry

            lax.fori_loop(0, rows // big, gather, 0)

        return carry

    lax.fori_loop(0, 2 * STOPS, step, 0)
    for h in range(2):
        state_out[pl.ds(h * chunk, chunk), :] = sent[2 * STOPS - 2 + h]

    def turned(c, carry):
        here = pl.ds(pl.multiple_of(c * block, block), block)
        grad_out[here, :] = acc[:, here].T.astype(BF)
        return carry

    lax.fori_loop(0, rows // block, turned, 0)
    grad_out[rows:, :] = jnp.zeros((grad_out.shape[0] - rows, width), BF)

    def drained(t, carry):
        hop(t).wait_send()
        return carry

    lax.fori_loop(0, 2 * STOPS - 2, drained, 0)


def run_stops(queries, packed, entities):
    padded, width = queries.shape
    rows = packed.shape[2]
    part = entities.shape[0]
    chunk = part // 2
    vmem = pl.BlockSpec(memory_space=pltpu.VMEM)
    hops = 2 * STOPS
    return pl.pallas_call(
        stops_kernel,
        out_shape=(
            jax.ShapeDtypeStruct((part, width), F32),
            jax.ShapeDtypeStruct((padded, width), BF),
        ),
        in_specs=[vmem, vmem, pl.BlockSpec(memory_space=pl.ANY)],
        out_specs=(vmem, vmem),
        scratch_shapes=[
            pltpu.VMEM((hops, chunk, width), F32),
            pltpu.VMEM((hops, chunk, width), F32),
            pltpu.VMEM((part, width), BF),
            pltpu.VMEM((width, part), BF),
            pltpu.VMEM((part, rows), BF),
            pltpu.VMEM((width, rows), F32),
            pltpu.SemaphoreType.DMA((2,)),
            pltpu.SemaphoreType.DMA((hops,)),
            pltpu.SemaphoreType.DMA((hops,)),
        ],
        compiler_params=pltpu.CompilerParams(
            collective_id=2, has_side_effects=True, vmem_limit_bytes=28 << 20
        ),
        name="run_stops",
    )(queries, packed, entities)


def add_into(dst, *others):
    lead = dst.shape[:-2]
    total = 1
    for n in lead:
        total *= n

    def body(i, carry):
        index, rest = [], i
        for n in reversed(lead):
            index.insert(0, lax.rem(rest, n))
            rest = rest // n
        value = dst[tuple(index)].astype(F32)
        for other in others:
            value = value + other[tuple(index)].astype(F32)
        dst[tuple(index)] = value.astype(dst.dtype)
        return carry

    lax.fori_loop(0, total, body, 0)


class Ring:
    def __init__(self, mail, place, ahead, behind, piece, halves, land_half, land_full):
        self.mail, self.place, self.ahead, self.behind = mail, place, ahead, behind
        self.piece, self.halves, self.land_half, self.land_full = piece, halves, land_half, land_full

    def one(self):
        far = turn(self.place, 2)
        self.h = [
            self.mail.send(self.halves(self.piece(far))[d], self.land_half[d], device)
            for d, device in enumerate((self.ahead, self.behind))
        ]

    def two(self):
        self.f = []
        for d, (step, device) in enumerate(((1, self.ahead), (3, self.behind))):
            self.h[d].wait_recv()
            target = self.piece(turn(self.place, step))
            add_into(self.halves(target)[d], self.land_half[d])
            self.f.append(self.mail.send(target, self.land_full[d], device))

    def three(self):
        for copy in self.f:
            copy.wait_recv()
        return self.piece(self.place), self.land_full


def scatter_kernel(
    place, terms, back, out, source_grad, got,
    ax_h, ax_f, ay_h, ay_f, az_h, az_f, by_h, by_f, bx_h, bx_f, bz_h, bz_f, swap_send, swap_recv, send_sem, recv_sem
):
    at = Spot()
    mail = Mail(send_sem, recv_sem)
    partner = at.device(core=1 - at.core)
    xs = at.device(x=turn(at.x, 1)), at.device(x=turn(at.x, 3))
    ys = at.device(y=turn(at.y, 1)), at.device(y=turn(at.y, 3))
    zs = at.device(z=turn(at.z, 1)), at.device(z=turn(at.z, 3))
    greet([partner, *xs, *ys, *zs])

    def swap(j, r):
        zh, x = r // 4, lax.rem(r, 4)
        return pltpu.make_async_remote_copy(
            src_ref=terms.at[j, zh, x, :, :, 1 - at.core],
            dst_ref=got.at[j, zh, x],
            send_sem=swap_send.at[j, r],
            recv_sem=swap_recv.at[j, r],
            device_id=partner,
            device_id_type=MESH,
        )

    def offer(i, carry):
        swap(i // 8, lax.rem(i, 8)).start()
        return carry

    lax.fori_loop(0, 16, offer, 0)

    def joined(j):
        def one(r, carry):
            swap(j, r).wait_recv()
            zh, x = r // 4, lax.rem(r, 4)
            add_into(got.at[j, zh, x], terms.at[j, zh, x, :, :, at.core])
            return carry

        lax.fori_loop(0, 8, one, 0)

    def unsort(begin, end):
        lanes = 128
        total = place.shape[1]

        def one(b, carry):
            here = pl.ds(pl.multiple_of(b * lanes, lanes), lanes)
            mine = jnp.broadcast_to(place[:, here], (lanes, lanes)).T
            index = lax.broadcasted_iota(jnp.int32, (lanes, lanes), 1)
            choose = jnp.concatenate(
                [(mine == index + t * lanes).astype(F32).astype(BF) for t in range(total // lanes)], axis=1
            )
            source_grad[here, :] = jnp.dot(choose, back[0:total, :], preferred_element_type=F32).astype(BF)
            return carry

        lax.fori_loop(begin, end, one, 0)


    def first_half(ref):
        return ref.at[0], ref.at[1]

    def row_halves(ref):
        rows = ref.shape[0] // 2
        return ref.at[pl.ds(0, rows)], ref.at[pl.ds(rows, rows)]

    def two(ref):
        return ref.at[0], ref.at[1]

    a, b = got.at[0], got.at[1]
    ax = Ring(mail, at.x, *xs, lambda t: a.at[:, t], first_half, two(ax_h), two(ax_f))
    a1 = lambda: a.at[:, at.x]
    ay = Ring(mail, at.y, *ys, lambda t: a1().at[:, :, t], first_half, two(ay_h), two(ay_f))
    a2 = lambda z: a.at[z // 2, at.x, lax.rem(z, 2), at.y]
    az = Ring(mail, at.z, *zs, a2, row_halves, two(az_h), two(az_f))
    by = Ring(mail, at.y, *ys, lambda t: b.at[:, :, :, t], first_half, two(by_h), two(by_f))
    bx = Ring(mail, at.x, *xs, lambda t: b.at[:, t, :, at.y], first_half, two(bx_h), two(bx_f))
    b2 = lambda z: b.at[z // 2, at.x, lax.rem(z, 2), at.y]
    bz = Ring(mail, at.z, *zs, b2, row_halves, two(bz_h), two(bz_f))

    for j, ring in enumerate((ax, by)):
        joined(j)
        ring.one()
    unsort(0, 4)
    ax.two()
    by.two()
    unsort(4, 12)
    for ring, following in ((ax, ay), (by, bx)):
        piece, landed = ring.three()
        add_into(piece, *landed)
        following.one()
    unsort(12, 14)
    ay.two()
    bx.two()
    unsort(14, 16)
    for ring, following in ((ay, az), (bx, bz)):
        piece, landed = ring.three()
        add_into(piece, *landed)
        following.one()
    az.two()
    bz.two()
    for j, ring in enumerate((az, bz)):
        piece, landed = ring.three()
        out[:, j, :] = piece[...].astype(F32) + landed[0][...].astype(F32) + landed[1][...].astype(F32)

    def sent(i, carry):
        swap(i // 8, lax.rem(i, 8)).wait_send()
        return carry

    lax.fori_loop(0, 16, sent, 0)
    mail.drain()


def scatter_grads(place, terms, back):
    width = back.shape[1]
    total = place.shape[1]
    rows = width // 16
    terms = terms.reshape(2, 2, 4, 2, 4, 2, rows, width)
    v = lambda *lead: pltpu.VMEM((*lead, rows, width), BF)
    z = lambda r: pltpu.VMEM((2, r, width), BF)
    vmem = pl.BlockSpec(memory_space=pltpu.VMEM)
    return pl.pallas_call(
        scatter_kernel,
        out_shape=(jax.ShapeDtypeStruct((rows, 2, width), F32), jax.ShapeDtypeStruct((total, width), BF)),
        in_specs=[vmem, vmem, vmem],
        out_specs=(vmem, vmem),
        scratch_shapes=[
            v(2, 2, 4, 2, 4),
            v(2, 2, 4), v(2, 2, 2, 4), v(2, 2), v(2, 2, 2), z(rows // 2), v(2),
            v(2, 4, 2), v(2, 2, 4, 2), v(2, 2), v(2, 2, 2), z(rows // 2), v(2),
            pltpu.SemaphoreType.DMA((2, 8)),
            pltpu.SemaphoreType.DMA((2, 8)),
            pltpu.SemaphoreType.DMA((24,)),
            pltpu.SemaphoreType.DMA((24,)),
        ],
        compiler_params=pltpu.CompilerParams(
            collective_id=1, has_side_effects=True, vmem_limit_bytes=30 << 20
        ),
        name="scatter_grads",
    )(place, terms, back)


def shards(source_rows, rel_ids, relations, entities, pos_slot, negatives):
    rows = source_rows.shape[0]
    matrices, sorted_rows, packed, place, starts = gather_relations(
        relations,
        rel_ids.reshape(1, rows),
        source_rows,
        jnp.transpose(negatives, (0, 2, 1)),
        pos_slot.reshape(1, rows),
    )
    queries = make_queries(starts, sorted_rows, matrices)
    state, query_grad = run_stops(queries, packed, entities)
    back, terms = make_grads(starts, sorted_rows, query_grad, matrices)
    relation_grad, source_grad = scatter_grads(place, terms, back)
    return (state, source_grad, relation_grad)


def solution(mesh):
    placed = (
        P(("cand", "rel"), None),
        P(("cand", "rel"), None),
        P("rel", None, None),
        P(("cand", "rel"), None),
        P(("cand", "rel")),
        P(None, ("cand", "rel"), None),
    )
    return jax.shard_map(
        shards,
        mesh=mesh,
        in_specs=placed,
        out_specs=(P(("cand", "rel"), None), P(("cand", "rel"), None), P("cand", "rel", None)),
        check_vma=False,
    )
```

time: 201 us -> 161 us (0.80)
  Pallas kernels: 181 us -> 152 us
  local copies, waits for them, and re-layouts: 19 us -> 8.31 us
    pallas_call x2, Pallas kernels: 74.8 us -> 54.8 us  [the longest x1 44 us: scatter_grads(): pl.pallas_call(scatter_kernel, out_shape=(jax.ShapeDtypeStruct((rows, 2,...]
    unnamed x26 -> x15, local copies, waits for them, and re-layouts: 18.9 us -> 8.2 us
    pallas_call x1, Pallas kernels: 59.9 us -> 50 us  [run_stops(): pl.pallas_call(stops_kernel, out_shape=(jax.ShapeDtypeStruct((part, width...]
where the time goes in v3:
time: 161 us
  Pallas kernels  152 us (94%)
  local copies, waits for them, and re-layouts  8.31 us (5%)
    pallas_call x1, Pallas kernels, run_stops(): pl.pallas_call(stops_kernel, out_shape=(jax.ShapeDtypeStruct((part, width...  50 us
    pallas_call x1, Pallas kernels, scatter_grads(): pl.pallas_call(scatter_kernel, out_shape=(jax.ShapeDtypeStruct((rows, 2,...  44 us
    pallas_call x1, Pallas kernels, gather_relations(): pl.pallas_call(gather_kernel, out_shape=(jax.ShapeDtypeStruct((owners, pe...  41.1 us
    pallas_call x1, Pallas kernels, make_grads(): pl.pallas_call(group_grads, out_shape=(jax.ShapeDtypeStruct(grads.shape,...  10.8 us
    unnamed x15, local copies, waits for them, and re-layouts  8.2 us
    pallas_call x1, Pallas kernels, make_queries(): pl.pallas_call(group_queries, out_shape=jax.ShapeDtypeStruct(rows.shape,...  5.73 us

profile of v3, /device:TPU:0, one launch (start us, length us, event | category | flops | bytes accessed | tf_op | source)
XLA Modules:
  0.0 160.7 jit_solution(15600021862126382184)
XLA Ops:
  0.6 0.0 copy-start
  0.6 1.6 copy-done
  2.2 0.0 copy-start.1
  2.2 1.2 copy-done.1
  3.4 0.0 copy-start.2
  3.5 1.2 copy-done.2
  4.7 0.0 copy-start.4
  4.7 0.7 copy-done.4
  5.4 0.0 copy-start.5
  5.4 0.7 copy-done.5
  6.1 41.1 %gather_relations.1 = (bf16[8,2,512,512]{3,2,1,0:T(8,128)(2,1)S(1)}, bf16[2320,512]{1,0:T(8,128)(2,1)S(1)}, s32[8,64,2048]{2,1,0:T(8,128)S(1)}, s32[1,2048]{1,0:T(1,128)S(1)}, s32[16,128]{1,0:T(8,128)S(1)}) custom-call(bf16[2,512,512]{2,1,0:T(8,128)(2,1)S(1)} %copy-done.1, s32[1,2048]{1,0:T(1,128)S(1)} %bitcast.9, bf16[2048,512]{1,0:T(8,128)(2,1)S(1)} %copy-done, ...), custom_call_target="tpu_custom_call" | custom-call | tf_op jit(solution)/shard_map/gather_relations/pallas_call | solution.py:375
  47.2 0.1 slice_reduce_fusion
  47.3 0.1 pad_add_fusion.starts
  47.4 0.0 copy-start.3
  47.4 5.7 %make_queries.1.q = bf16[2320,512]{1,0:T(8,128)(2,1)S(1)} custom-call(s32[17]{0:T(128)S(1)} %pad_add_fusion.starts, bf16[2320,512]{1,0:T(8,128)(2,1)S(1)} %get-tuple-element.15.rows_ref, bf16[16,512,512]{2,1,0:T(8,128)(2,1)S(1)} %bitcast.5), custom_call_target="tpu_custom_call" | custom-call | tf_op jit(solution)/shard_map/make_queries/pallas_call | solution.py:127
  53.1 0.0 copy-done.3
  53.1 50.0 %run_stops.1 = (f32[256,512]{1,0:T(8,128)S(1)}, bf16[2320,512]{1,0:T(8,128)(2,1)S(1)}) custom-call(bf16[2320,512]{1,0:T(8,128)(2,1)S(1)} %make_queries.1.q, s32[8,64,2048]{2,1,0:T(8,128)S(1)} %get-tuple-element.17.packed, f32[256,512]{1,0:T(8,128)S(1)} %copy-done.3), custom_call_target="tpu_custom_call" | custom-call | tf_op jit(solution)/shard_map/run_stops/pallas_call | solution.py:517
  103.1 10.8 %make_grads.1 = (bf16[2320,512]{1,0:T(8,128)(2,1)S(1)}, bf16[2,8,512,512]{3,2,1,0:T(8,128)(2,1)S(1)}) custom-call(s32[17]{0:T(128)S(1)} %pad_add_fusion.starts, bf16[2320,512]{1,0:T(8,128)(2,1)S(1)} %get-tuple-element.15.rows_ref, bf16[2320,512]{1,0:T(8,128)(2,1)S(1)} %get-tuple-element.20.grads, bf16[16,512,512]{2,1,0:T(8,128)(2,1)S(1)} %bitcast.6), custom_call_target="tpu_custom_call" | custom-call | tf_op jit(solution)/shard_map/make_grads/pallas_call | solution.py:157
  114.0 44.0 %scatter_grads.1 = (f32[32,2,512]{2,1,0:T(2,128)S(1)}, bf16[2048,512]{1,0:T(8,128)(2,1)S(1)}) custom-call(s32[1,2048]{1,0:T(1,128)S(1)} %get-tuple-element.19.place, bf16[2,2,4,2,4,2,32,512]{7,6,5,4,3,2,1,0:T(8,128)(2,1)S(1)} %bitcast.7, bf16[2320,512]{1,0:T(8,128)(2,1)S(1)} %get-tuple-element.22.back), custom_call_target="tpu_custom_call" | custom-call | tf_op jit(solution)/shard_map/scatter_grads/pallas_call | solution.py:706
  158.0 0.8 copy.12
  158.8 1.3 copy.13
  160.1 0.7 copy.14
Async XLA Ops:
  0.6 1.6 copy-start
  2.2 1.2 copy-start.1
  3.4 1.2 copy-start.2
  4.7 0.7 copy-start.4
  5.4 0.7 copy-start.5
  47.4 5.7 %copy-start.3 = (f32[256,512]{1,0:T(8,128)S(1)}, f32[256,512]{1,0:T(8,128)}, u32[]{:S(2)}) copy-start(f32[256,512]{1,0:T(8,128)} %entities.1) | copy-start | bytes 1572868

commit v4 on v3

--- a/solution.py
+++ b/solution.py
@@ -206,8 +206,9 @@
 
 
 def gather_kernel(
-    own, ids, rows_ref, picks, target, out, rows_out, packed, place_out, starts_out,
-    meta, sorted_picks, sorted_target, low, unit, local_sem, send_sem, recv_sem,
+    own_in, ids_in, rows_in, picks_in, target_in, out, rows_out, packed, place_out, starts_out,
+    own, ids, rows_ref, picks, target,
+    meta, sorted_picks, sorted_target, low, unit, local_sem, fetch_sem, send_sem, recv_sem,
 ):
     at = Spot()
     mail = Mail(send_sem, recv_sem)
@@ -215,7 +216,16 @@
     down, up = at.device(y=turn(at.y, 3)), at.device(y=turn(at.y, 1))
     across = at.device(z=3 - at.z)
     partner = at.device(core=1 - at.core)
+    fetch = [
+        pltpu.make_async_copy(source, landing, fetch_sem.at[i])
+        for i, (source, landing) in enumerate(
+            ((own_in, own), (ids_in, ids), (target_in, target), (picks_in, picks), (rows_in, rows_ref))
+        )
+    ]
+    for copy in fetch:
+        copy.start()
     greet([left, right, down, up, across, partner])
+    fetch[0].wait()
     half = own.shape[1] // 2
     share = half // 4
 
@@ -267,6 +277,8 @@
     stops, samples, total = picks.shape
     part = total // stops
     nrel = starts_out.shape[0]
+    for copy in fetch[1:]:
+        copy.wait()
     place, starts = sort_plan(ids[...], nrel)
     place = place.astype(jnp.int32)
     place_out[...] = place
@@ -381,15 +393,17 @@
             jax.ShapeDtypeStruct((1, total), jnp.int32),
             jax.ShapeDtypeStruct((nrel, 128), jnp.int32),
         ),
-        in_specs=[vmem] * 5,
+        in_specs=[pl.BlockSpec(memory_space=pltpu.HBM)] * 5,
         out_specs=(pl.BlockSpec(memory_space=pl.ANY), *[vmem] * 4),
         scratch_shapes=[
+            *(pltpu.VMEM(a.shape, a.dtype) for a in (relations, ids, rows, picks, target)),
             pltpu.VMEM((stops * samples + 16, total), BF),
             pltpu.VMEM((stops * samples, total), jnp.int32),
             pltpu.VMEM((1, total), jnp.int32),
             pltpu.VMEM((24, total), jnp.int32),
             pltpu.VMEM((24, total), jnp.int32),
             pltpu.SemaphoreType.DMA((2,)),
+            pltpu.SemaphoreType.DMA((5,)),
             pltpu.SemaphoreType.DMA((36,)),
             pltpu.SemaphoreType.DMA((36,)),
         ],
@@ -405,10 +419,12 @@
 
 STOPS = 8
 learn_rate = 0.005
+LOG2E = 1.4426950408889634
 
 
 def stops_kernel(
-    q, packed, entities, state_out, grad_out, held, sent, wide, turned_wide, weights, acc, local_sem, send_sem, recv_sem
+    q, packed, entities, state_out, grad_out, held, sent, held_short, sent_short, now, wide, turned_wide, weights, acc,
+    local_sem, send_sem, recv_sem,
 ):
     cand, rel = lax.axis_index("cand"), lax.axis_index("rel")
     n = lax.axis_size("cand")
@@ -429,27 +445,39 @@
     for copy in fetch:
         copy.wait()
 
-    def hop(t):
-        return pltpu.make_async_remote_copy(
-            src_ref=sent.at[t],
-            dst_ref=held.at[t + 2],
-            send_sem=send_sem.at[t],
-            recv_sem=recv_sem.at[t],
+    def copier(kind, source, landing):
+        return lambda t: pltpu.make_async_remote_copy(
+            src_ref=source.at[t],
+            dst_ref=landing.at[t + 2],
+            send_sem=send_sem.at[kind, t],
+            recv_sem=recv_sem.at[kind, t],
             device_id=ahead,
             device_id_type=MESH,
         )
+
+    core = lax.rem(cand, 2)
+    hop, hop_short = copier(0, sent, held), copier(1, sent_short, held_short)
 
     def step(t, carry):
         half = lax.rem(t, 2)
         stop = t // 2
         here_rows = pl.ds(pl.multiple_of(half * chunk, chunk), chunk)
 
-        @pl.when(t >= 2)
+        @pl.when(t < 2)
+        def _():
+            now[...] = held[t]
+
+        @pl.when((t >= 2) & (core == 1))
         def _():
             hop(t - 2).wait_recv()
-
-        state = held[t]
-        rounded = state.astype(BF)
+            now[...] = held[t]
+
+        @pl.when((t >= 2) & (core == 0))
+        def _():
+            hop_short(t - 2).wait_recv()
+            now[...] = held_short[t].astype(F32)
+
+        rounded = now[...].astype(BF)
         wide[here_rows, :] = rounded
         pieces = []
         for i in range(rows // block):
@@ -462,17 +490,23 @@
                 [lax.shift_right_logical(marks, 16 * half + 8 * p) for p in range(chunk // LOW)], axis=0
             )
             named = lax.bitwise_and(marks, 31).astype(F32)
-            chance = 1.0 / (1.0 + jnp.exp(-logits))
+            chance = 1.0 / (1.0 + jnp.exp2(logits * -LOG2E))
             product = named * chance
             pieces.append(jnp.where(lax.bitwise_and(marks, 32) != 0, product - 1.0, product).astype(BF))
         weight = jnp.concatenate(pieces, axis=1)
         weights[here_rows, :] = weight
         change = jnp.dot(weight, q[0:rows, :], preferred_element_type=F32)
-        sent[t] = state - learn_rate * change
-
-        @pl.when(t < 2 * STOPS - 2)
+        moved = now[...] - learn_rate * change
+        sent[t] = moved
+        sent_short[t] = moved.astype(BF)
+
+        @pl.when((t < 2 * STOPS - 2) & (core == 0))
         def _():
             hop(t).start()
+
+        @pl.when((t < 2 * STOPS - 2) & (core == 1))
+        def _():
+            hop_short(t).start()
 
         @pl.when(half == 1)
         def _():
@@ -484,7 +518,7 @@
                 acc[:, here] += jnp.dot(turned_wide[...], weights[:, here], preferred_element_type=F32)
                 return carry
 
-            lax.fori_loop(0, rows // big, gather, 0)
+            lax.fori_loop(0, rows // big, gather, 0, unroll=True)
 
         return carry
 
@@ -501,7 +535,14 @@
     grad_out[rows:, :] = jnp.zeros((grad_out.shape[0] - rows, width), BF)
 
     def drained(t, carry):
-        hop(t).wait_send()
+        @pl.when(core == 0)
+        def _():
+            hop(t).wait_send()
+
+        @pl.when(core == 1)
+        def _():
+            hop_short(t).wait_send()
+
         return carry
 
     lax.fori_loop(0, 2 * STOPS - 2, drained, 0)
@@ -520,18 +561,21 @@
             jax.ShapeDtypeStruct((part, width), F32),
             jax.ShapeDtypeStruct((padded, width), BF),
         ),
-        in_specs=[vmem, vmem, pl.BlockSpec(memory_space=pl.ANY)],
+        in_specs=[vmem, vmem, pl.BlockSpec(memory_space=pltpu.HBM)],
         out_specs=(vmem, vmem),
         scratch_shapes=[
             pltpu.VMEM((hops, chunk, width), F32),
             pltpu.VMEM((hops, chunk, width), F32),
+            pltpu.VMEM((hops, chunk, width), BF),
+            pltpu.VMEM((hops, chunk, width), BF),
+            pltpu.VMEM((chunk, width), F32),
             pltpu.VMEM((part, width), BF),
             pltpu.VMEM((width, part), BF),
             pltpu.VMEM((part, rows), BF),
             pltpu.VMEM((width, rows), F32),
             pltpu.SemaphoreType.DMA((2,)),
-            pltpu.SemaphoreType.DMA((hops,)),
-            pltpu.SemaphoreType.DMA((hops,)),
+            pltpu.SemaphoreType.DMA((2, hops)),
+            pltpu.SemaphoreType.DMA((2, hops)),
         ],
         compiler_params=pltpu.CompilerParams(
             collective_id=2, has_side_effects=True, vmem_limit_bytes=28 << 20

time: 161 us -> 147 us (0.913)
  Pallas kernels: 152 us -> 138 us
    pallas_call x1, Pallas kernels: 50 us -> 32.2 us  [run_stops(): pl.pallas_call(stops_kernel, out_shape=(jax.ShapeDtypeStruct((part, width...]
    pallas_call x1, Pallas kernels: 44 us -> 47.5 us  [scatter_grads(): pl.pallas_call(scatter_kernel, out_shape=(jax.ShapeDtypeStruct((rows, 2,...]
where the time goes in v4:
time: 147 us
  Pallas kernels  138 us (94%)
  local copies, waits for them, and re-layouts  8.31 us (6%)
    pallas_call x1, Pallas kernels, scatter_grads(): pl.pallas_call(scatter_kernel, out_shape=(jax.ShapeDtypeStruct((rows, 2,...  47.5 us
    pallas_call x1, Pallas kernels, gather_relations(): pl.pallas_call(gather_kernel, out_shape=(jax.ShapeDtypeStruct((owners, pe...  41.5 us
    pallas_call x1, Pallas kernels, run_stops(): pl.pallas_call(stops_kernel, out_shape=(jax.ShapeDtypeStruct((part, width...  32.2 us
    pallas_call x1, Pallas kernels, make_grads(): pl.pallas_call(group_grads, out_shape=(jax.ShapeDtypeStruct(grads.shape,...  10.8 us
    unnamed x15, local copies, waits for them, and re-layouts  8.2 us
    pallas_call x1, Pallas kernels, make_queries(): pl.pallas_call(group_queries, out_shape=jax.ShapeDtypeStruct(rows.shape,...  5.73 us

profile of v4, /device:TPU:0, one launch (start us, length us, event | category | flops | bytes accessed | tf_op | source)
XLA Modules:
  0.0 146.7 jit_solution(4547949901891883376)
XLA Ops:
  0.6 0.0 copy-start
  0.6 1.6 %copy-done = bf16[2048,512]{1,0:T(8,128)(2,1)S(1)} copy-done((bf16[2048,512]{1,0:T(8,128)(2,1)S(1)}, bf16[2048,512]{1,0:T(8,128)(2,1)}, u32[]{:S(2)}) %copy-start) | copy-done | bytes 2097176
  2.2 0.0 copy-start.1
  2.2 1.2 copy-done.1
  3.4 0.0 copy-start.2
  3.5 1.2 copy-done.2
  4.7 0.0 copy-start.4
  4.7 0.7 copy-done.4
  5.4 0.0 copy-start.5
  5.4 0.7 copy-done.5
  6.1 41.5 %gather_relations.1 = (bf16[8,2,512,512]{3,2,1,0:T(8,128)(2,1)S(1)}, bf16[2320,512]{1,0:T(8,128)(2,1)S(1)}, s32[8,64,2048]{2,1,0:T(8,128)S(1)}, s32[1,2048]{1,0:T(1,128)S(1)}, s32[16,128]{1,0:T(8,128)S(1)}) custom-call(bf16[2,512,512]{2,1,0:T(8,128)(2,1)S(1)} %copy-done.1, s32[1,2048]{1,0:T(1,128)S(1)} %bitcast.9, bf16[2048,512]{1,0:T(8,128)(2,1)S(1)} %copy-done, ...), custom_call_target="tpu_custom_call" | custom-call | tf_op jit(solution)/shard_map/gather_relations/pallas_call | solution.py:387
  47.6 0.1 slice_reduce_fusion
  47.7 0.1 pad_add_fusion.starts
  47.8 0.0 copy-start.3
  47.8 5.7 %make_queries.1.q = bf16[2320,512]{1,0:T(8,128)(2,1)S(1)} custom-call(s32[17]{0:T(128)S(1)} %pad_add_fusion.starts, bf16[2320,512]{1,0:T(8,128)(2,1)S(1)} %get-tuple-element.15.rows_ref, bf16[16,512,512]{2,1,0:T(8,128)(2,1)S(1)} %bitcast.5), custom_call_target="tpu_custom_call" | custom-call | tf_op jit(solution)/shard_map/make_queries/pallas_call | solution.py:127
  53.5 0.0 copy-done.3
  53.5 32.2 %run_stops.1 = (f32[256,512]{1,0:T(8,128)S(1)}, bf16[2320,512]{1,0:T(8,128)(2,1)S(1)}) custom-call(bf16[2320,512]{1,0:T(8,128)(2,1)S(1)} %make_queries.1.q, s32[8,64,2048]{2,1,0:T(8,128)S(1)} %get-tuple-element.17.packed, f32[256,512]{1,0:T(8,128)S(1)} %copy-done.3), custom_call_target="tpu_custom_call" | custom-call | tf_op jit(solution)/shard_map/run_stops/pallas_call | solution.py:558
  85.7 10.8 %make_grads.1 = (bf16[2320,512]{1,0:T(8,128)(2,1)S(1)}, bf16[2,8,512,512]{3,2,1,0:T(8,128)(2,1)S(1)}) custom-call(s32[17]{0:T(128)S(1)} %pad_add_fusion.starts, bf16[2320,512]{1,0:T(8,128)(2,1)S(1)} %get-tuple-element.15.rows_ref, bf16[2320,512]{1,0:T(8,128)(2,1)S(1)} %get-tuple-element.20.grads, bf16[16,512,512]{2,1,0:T(8,128)(2,1)S(1)} %bitcast.6), custom_call_target="tpu_custom_call" | custom-call | tf_op jit(solution)/shard_map/make_grads/pallas_call | solution.py:157
  96.5 47.5 %scatter_grads.1 = (f32[32,2,512]{2,1,0:T(2,128)S(1)}, bf16[2048,512]{1,0:T(8,128)(2,1)S(1)}) custom-call(s32[1,2048]{1,0:T(1,128)S(1)} %get-tuple-element.19.place, bf16[2,2,4,2,4,2,32,512]{7,6,5,4,3,2,1,0:T(8,128)(2,1)S(1)} %bitcast.7, bf16[2320,512]{1,0:T(8,128)(2,1)S(1)} %get-tuple-element.22.back), custom_call_target="tpu_custom_call" | custom-call | tf_op jit(solution)/shard_map/scatter_grads/pallas_call | solution.py:750
  144.0 0.8 copy.12
  144.8 1.3 copy.13
  146.1 0.7 copy.14
Async XLA Ops:
  0.6 1.6 %copy-start = (bf16[2048,512]{1,0:T(8,128)(2,1)S(1)}, bf16[2048,512]{1,0:T(8,128)(2,1)}, u32[]{:S(2)}) copy-start(bf16[2048,512]{1,0:T(8,128)(2,1)} %rows_in.1) | copy-start | bytes 6291460
  2.2 1.2 copy-start.1
  3.4 1.2 copy-start.2
  4.7 0.7 copy-start.4
  5.4 0.7 copy-start.5
  47.8 5.7 %copy-start.3 = (f32[256,512]{1,0:T(8,128)S(1)}, f32[256,512]{1,0:T(8,128)}, u32[]{:S(2)}) copy-start(f32[256,512]{1,0:T(8,128)} %entities.1) | copy-start | bytes 1572868

commit v5 on v4

--- a/solution.py
+++ b/solution.py
@@ -247,12 +247,8 @@
     me, far = at.zh * 4, (1 - at.zh) * 4
     x0, x1, x2, x3 = at.x, turn(at.x, 1), turn(at.x, 2), turn(at.x, 3)
     y0, y1, y2, y3 = at.y, turn(at.y, 1), turn(at.y, 2), turn(at.y, 3)
-    here = [
-        pltpu.make_async_copy(own.at[0], out.at[at.rel, 0], local_sem.at[0]),
-        pltpu.make_async_copy(own.at[1, quarter(y0)], out.at[at.rel, 1, quarter(y0)], local_sem.at[1]),
-    ]
-    for copy in here:
-        copy.start()
+    here = pltpu.make_async_copy(own, out.at[at.rel], local_sem)
+    here.start()
 
     def same(ref, device):
         return mail.send(ref, ref, device)
@@ -263,8 +259,23 @@
     def b(base, x, rows):
         return out.at[base + x, 1, rows]
 
-    def b4(base, rows):
-        return out.at[pl.ds(base, 4), 1, rows]
+    gifts = []
+
+    class Quarter:
+        def __init__(self, base, x):
+            self.base, self.x = base, x
+            self.sent = [same(b(base, x, quarter(y0)), device) for device in (up, down)]
+
+        def on(self):
+            self.sent[0].wait_recv()
+            first = same(b(self.base, self.x, quarter_halves(y3)[0]), up)
+            self.sent[1].wait_recv()
+            self.sent = [first, same(b(self.base, self.x, quarter_halves(y1)[1]), down)]
+
+        def done(self):
+            for copy in self.sent:
+                copy.wait_recv()
+            gifts.append(same(b(self.base, self.x, mine), partner))
 
     own_a, own_b = own.at[0, mine], own.at[1, quarter(y0)]
     b_across = mail.send(own_b, b(me, x0, quarter(y0)), across)
@@ -298,74 +309,78 @@
     def count(s):
         tally(s, part, sorted_picks, sorted_target, low, unit, packed)
 
+    h0, h1 = quarter_halves(y0)
     work(0)
-    h0, h1 = quarter_halves(y0)
     b_right.wait_recv()
     b_on_right = same(b(me, x3, h0), right)
+    q_me3 = Quarter(me, x3)
     b_left.wait_recv()
     b_on_left = same(b(me, x1, h1), left)
+    q_me1 = Quarter(me, x1)
     b_across.wait_recv()
     b_far_right = same(b(far, x0, quarter(y0)), right)
     b_far_left = same(b(far, x0, quarter(y0)), left)
+    q_far0 = Quarter(far, x0)
     work(1)
     a_right.wait_recv()
     a_on_right = same(a(me, x3, first), right)
-    gifts = [same(a(me, x3, mine), partner)]
+    gifts.append(same(a(me, x3, mine), partner))
     a_left.wait_recv()
     a_on_left = same(a(me, x1, second), left)
     gifts.append(same(a(me, x1, mine), partner))
-    work(2)
     b_on_right.wait_recv()
     b_on_left.wait_recv()
-    here[1].wait()
-    me_up, me_down = same(b4(me, quarter(y0)), up), same(b4(me, quarter(y0)), down)
+    q_me2 = Quarter(me, x2)
+    work(2)
     b_far_right.wait_recv()
     b_far_on_right = same(b(far, x3, h0), right)
+    q_far3 = Quarter(far, x3)
     b_far_left.wait_recv()
     b_far_on_left = same(b(far, x1, h1), left)
-    work(3)
+    q_far1 = Quarter(far, x1)
     a_across.wait_recv()
     a_far_right = same(a(far, x0, mine), right)
     a_far_left = same(a(far, x0, mine), left)
     gifts.append(same(a(far, x0, mine), partner))
+    work(3)
+    q_me3.on()
+    q_me1.on()
     work(4)
-    b_far_on_right.wait_recv()
-    b_far_on_left.wait_recv()
-    far_up, far_down = same(b4(far, quarter(y0)), up), same(b4(far, quarter(y0)), down)
+    q_far0.on()
     a_on_right.wait_recv()
     a_opposite = [same(a(me, x2, first), across)]
     a_on_left.wait_recv()
     a_opposite.append(same(a(me, x2, second), across))
     gifts.append(same(a(me, x2, mine), partner))
+    b_far_on_right.wait_recv()
+    b_far_on_left.wait_recv()
+    q_far2 = Quarter(far, x2)
     work(5)
-    me_up.wait_recv()
-    me_on_up = same(b4(me, quarter_halves(y3)[0]), up)
-    me_down.wait_recv()
-    me_on_down = same(b4(me, quarter_halves(y1)[1]), down)
+    q_me2.on()
+    q_me3.done()
     work(6)
+    q_far3.on()
+    q_me1.done()
     work(7)
+    q_far1.on()
+    q_far0.done()
     count(0)
-    far_up.wait_recv()
-    far_on_up = same(b4(far, quarter_halves(y3)[0]), up)
-    far_down.wait_recv()
-    far_on_down = same(b4(far, quarter_halves(y1)[1]), down)
+    q_far2.on()
+    q_me2.done()
     count(1)
     a_far_right.wait_recv()
     gifts.append(same(a(far, x3, mine), partner))
     a_far_left.wait_recv()
     gifts.append(same(a(far, x1, mine), partner))
+    q_far3.done()
     count(2)
-    me_on_up.wait_recv()
-    me_on_down.wait_recv()
-    gifts.append(same(b4(me, mine), partner))
     for copy in a_opposite:
         copy.wait_recv()
     gifts.append(same(a(far, x2, mine), partner))
+    q_far1.done()
+    q_far2.done()
     count(3)
     count(4)
-    far_on_up.wait_recv()
-    far_on_down.wait_recv()
-    gifts.append(same(b4(far, mine), partner))
 
     def later(s, carry):
         count(s)
@@ -375,7 +390,7 @@
     for copy in gifts:
         copy.wait_recv()
     mail.drain()
-    here[0].wait()
+    here.wait()
 
 
 def gather_relations(relations, ids, rows, picks, target):
@@ -402,10 +417,10 @@
             pltpu.VMEM((1, total), jnp.int32),
             pltpu.VMEM((24, total), jnp.int32),
             pltpu.VMEM((24, total), jnp.int32),
-            pltpu.SemaphoreType.DMA((2,)),
+            pltpu.SemaphoreType.DMA,
             pltpu.SemaphoreType.DMA((5,)),
-            pltpu.SemaphoreType.DMA((36,)),
-            pltpu.SemaphoreType.DMA((36,)),
+            pltpu.SemaphoreType.DMA((60,)),
+            pltpu.SemaphoreType.DMA((60,)),
         ],
         compiler_params=pltpu.CompilerParams(
             collective_id=0, has_side_effects=True, vmem_limit_bytes=24 << 20
@@ -585,7 +600,12 @@
 
 
 def add_into(dst, *others):
-    lead = dst.shape[:-2]
+    lead, size = [], dst.size
+    for n in dst.shape[:-2]:
+        if size <= 1 << 15:
+            break
+        lead.append(n)
+        size //= n
     total = 1
     for n in lead:
         total *= n
@@ -595,52 +615,108 @@
         for n in reversed(lead):
             index.insert(0, lax.rem(rest, n))
             rest = rest // n
-        value = dst[tuple(index)].astype(F32)
+        index = tuple(index) if index else ...
+        value = dst[index].astype(F32)
         for other in others:
-            value = value + other[tuple(index)].astype(F32)
-        dst[tuple(index)] = value.astype(dst.dtype)
+            value = value + other[index].astype(F32)
+        dst[index] = value.astype(dst.dtype)
         return carry
 
-    lax.fori_loop(0, total, body, 0)
-
-
-class Ring:
-    def __init__(self, mail, place, ahead, behind, piece, halves, land_half, land_full):
-        self.mail, self.place, self.ahead, self.behind = mail, place, ahead, behind
-        self.piece, self.halves, self.land_half, self.land_full = piece, halves, land_half, land_full
+    if total == 1:
+        body(0, 0)
+    else:
+        lax.fori_loop(0, total, body, 0)
+
+
+ORDERS = (("xyz", "yxz", "zxy", "xyz"), ("yxz", "xyz", "zyx", "yxz"))
+SIZES = {"zh": 2, "x": 4, "zl": 2, "y": 4}
+OF_AXIS = {"x": ("x",), "y": ("y",), "z": ("zh", "zl")}
+
+
+def piece_shape(order, phase, rows, columns):
+    gone = [name for axis in order[: phase + 1] for name in OF_AXIS[axis]]
+    free = [n for name, n in SIZES.items() if name not in gone]
+    if free:
+        return (free[0] // 2, *free[1:], rows, columns), (*free, rows, columns)
+    return (rows, columns // 2), (rows, columns)
+
+
+def landing_shapes(order, rows, columns):
+    shapes = []
+    for phase in range(3):
+        half, whole = piece_shape(order, phase, rows, columns)
+        shapes += [(2, *half), (2, *whole)]
+    return shapes
+
+
+class Eighth:
+    def __init__(self, mail, at, base, row, column, order, landings, ways):
+        self.mail, self.at, self.base, self.order, self.landings, self.ways = mail, at, base, order, landings, ways
+        self.row, self.column = row, column
+        self.fixed, self.phase = {}, 0
+
+    def view(self, fixed, cut=None):
+        index = []
+        free = [name for name in SIZES if name not in fixed]
+        for name, n in SIZES.items():
+            if name in fixed:
+                index.append(fixed[name])
+            elif cut is not None and name == free[0]:
+                index.append(pl.ds(cut * (n // 2), n // 2))
+            else:
+                index.append(slice(None))
+        start, size = self.column
+        if cut is not None and not free:
+            start, size = start + cut * (size // 2), size // 2
+        return self.base.at[(*index, pl.ds(*self.row), pl.ds(start, size))]
+
+    def spot(self, by):
+        axis = self.order[self.phase]
+        t = turn(getattr(self.at, axis), by)
+        return {**self.fixed, **({"zh": t // 2, "zl": lax.rem(t, 2)} if axis == "z" else {axis: t})}
 
     def one(self):
-        far = turn(self.place, 2)
+        self.half, self.whole = self.landings[2 * self.phase : 2 * self.phase + 2]
+        self.devices = self.ways[self.order[self.phase]]
         self.h = [
-            self.mail.send(self.halves(self.piece(far))[d], self.land_half[d], device)
-            for d, device in enumerate((self.ahead, self.behind))
+            self.mail.send(self.view(self.spot(2), d), self.half.at[d], device)
+            for d, device in enumerate(self.devices)
         ]
 
     def two(self):
         self.f = []
-        for d, (step, device) in enumerate(((1, self.ahead), (3, self.behind))):
+        for d, device in enumerate(self.devices):
             self.h[d].wait_recv()
-            target = self.piece(turn(self.place, step))
-            add_into(self.halves(target)[d], self.land_half[d])
-            self.f.append(self.mail.send(target, self.land_full[d], device))
+            target = self.spot((1, 3)[d])
+            add_into(self.view(target, d), self.half.at[d])
+            self.f.append(self.mail.send(self.view(target), self.whole.at[d], device))
 
     def three(self):
         for copy in self.f:
             copy.wait_recv()
-        return self.piece(self.place), self.land_full
-
-
-def scatter_kernel(
-    place, terms, back, out, source_grad, got,
-    ax_h, ax_f, ay_h, ay_f, az_h, az_f, by_h, by_f, bx_h, bx_f, bz_h, bz_f, swap_send, swap_recv, send_sem, recv_sem
-):
+        self.fixed = self.spot(0)
+        self.phase += 1
+        if self.phase < 3:
+            add_into(self.view(self.fixed), self.whole.at[0], self.whole.at[1])
+            self.one()
+
+    def result(self):
+        own = self.view(self.fixed)[...].astype(F32)
+        return own + self.whole[0].astype(F32) + self.whole[1].astype(F32)
+
+
+def scatter_kernel(place, terms, back, out, source_grad, got, *rest):
+    swap_send, swap_recv, send_sem, recv_sem = rest[-4:]
+    landings = rest[:-4]
     at = Spot()
     mail = Mail(send_sem, recv_sem)
     partner = at.device(core=1 - at.core)
-    xs = at.device(x=turn(at.x, 1)), at.device(x=turn(at.x, 3))
-    ys = at.device(y=turn(at.y, 1)), at.device(y=turn(at.y, 3))
-    zs = at.device(z=turn(at.z, 1)), at.device(z=turn(at.z, 3))
-    greet([partner, *xs, *ys, *zs])
+    ways = {
+        "x": (at.device(x=turn(at.x, 1)), at.device(x=turn(at.x, 3))),
+        "y": (at.device(y=turn(at.y, 1)), at.device(y=turn(at.y, 3))),
+        "z": (at.device(z=turn(at.z, 1)), at.device(z=turn(at.z, 3))),
+    }
+    greet([partner, *ways["x"], *ways["y"], *ways["z"]])
 
     def swap(j, r):
         zh, x = r // 4, lax.rem(r, 4)
@@ -685,51 +761,34 @@
         lax.fori_loop(begin, end, one, 0)
 
 
-    def first_half(ref):
-        return ref.at[0], ref.at[1]
-
-    def row_halves(ref):
-        rows = ref.shape[0] // 2
-        return ref.at[pl.ds(0, rows)], ref.at[pl.ds(rows, rows)]
-
-    def two(ref):
-        return ref.at[0], ref.at[1]
-
-    a, b = got.at[0], got.at[1]
-    ax = Ring(mail, at.x, *xs, lambda t: a.at[:, t], first_half, two(ax_h), two(ax_f))
-    a1 = lambda: a.at[:, at.x]
-    ay = Ring(mail, at.y, *ys, lambda t: a1().at[:, :, t], first_half, two(ay_h), two(ay_f))
-    a2 = lambda z: a.at[z // 2, at.x, lax.rem(z, 2), at.y]
-    az = Ring(mail, at.z, *zs, a2, row_halves, two(az_h), two(az_f))
-    by = Ring(mail, at.y, *ys, lambda t: b.at[:, :, :, t], first_half, two(by_h), two(by_f))
-    bx = Ring(mail, at.x, *xs, lambda t: b.at[:, t, :, at.y], first_half, two(bx_h), two(bx_f))
-    b2 = lambda z: b.at[z // 2, at.x, lax.rem(z, 2), at.y]
-    bz = Ring(mail, at.z, *zs, b2, row_halves, two(bz_h), two(bz_f))
-
-    for j, ring in enumerate((ax, by)):
+    rows, columns = got.shape[-2] // 2, got.shape[-1] // 2
+    units = [
+        [
+            Eighth(
+                mail, at, got.at[j], (u // 2 * rows, rows), (u % 2 * columns, columns), ORDERS[j][u],
+                landings[(4 * j + u) * 6 : (4 * j + u) * 6 + 6], ways,
+            )
+            for u in range(4)
+        ]
+        for j in range(2)
+    ]
+    every = [unit for group in units for unit in group]
+    for j in range(2):
         joined(j)
-        ring.one()
-    unsort(0, 4)
-    ax.two()
-    by.two()
-    unsort(4, 12)
-    for ring, following in ((ax, ay), (by, bx)):
-        piece, landed = ring.three()
-        add_into(piece, *landed)
-        following.one()
-    unsort(12, 14)
-    ay.two()
-    bx.two()
-    unsort(14, 16)
-    for ring, following in ((ay, az), (bx, bz)):
-        piece, landed = ring.three()
-        add_into(piece, *landed)
-        following.one()
-    az.two()
-    bz.two()
-    for j, ring in enumerate((az, bz)):
-        piece, landed = ring.three()
-        out[:, j, :] = piece[...].astype(F32) + landed[0][...].astype(F32) + landed[1][...].astype(F32)
+        for unit in units[j]:
+            unit.one()
+    unsort(0, 3)
+    for phase in range(3):
+        for unit in every:
+            unit.two()
+        unsort(3 + 4 * phase, 5 + 4 * phase)
+        for unit in every:
+            unit.three()
+        unsort(5 + 4 * phase, 7 + 4 * phase)
+    unsort(15, 16)
+    for j in range(2):
+        for u, unit in enumerate(units[j]):
+            out[unit.row[0] : unit.row[0] + rows, j, unit.column[0] : unit.column[0] + columns] = unit.result()
 
     def sent(i, carry):
         swap(i // 8, lax.rem(i, 8)).wait_send()
@@ -745,7 +804,6 @@
     rows = width // 16
     terms = terms.reshape(2, 2, 4, 2, 4, 2, rows, width)
     v = lambda *lead: pltpu.VMEM((*lead, rows, width), BF)
-    z = lambda r: pltpu.VMEM((2, r, width), BF)
     vmem = pl.BlockSpec(memory_space=pltpu.VMEM)
     return pl.pallas_call(
         scatter_kernel,
@@ -754,12 +812,16 @@
         out_specs=(vmem, vmem),
         scratch_shapes=[
             v(2, 2, 4, 2, 4),
-            v(2, 2, 4), v(2, 2, 2, 4), v(2, 2), v(2, 2, 2), z(rows // 2), v(2),
-            v(2, 4, 2), v(2, 2, 4, 2), v(2, 2), v(2, 2, 2), z(rows // 2), v(2),
+            *(
+                pltpu.VMEM(shape, BF)
+                for group in ORDERS
+                for order in group
+                for shape in landing_shapes(order, rows // 2, width // 2)
+            ),
             pltpu.SemaphoreType.DMA((2, 8)),
             pltpu.SemaphoreType.DMA((2, 8)),
-            pltpu.SemaphoreType.DMA((24,)),
-            pltpu.SemaphoreType.DMA((24,)),
+            pltpu.SemaphoreType.DMA((96,)),
+            pltpu.SemaphoreType.DMA((96,)),
         ],
         compiler_params=pltpu.CompilerParams(
             collective_id=1, has_side_effects=True, vmem_limit_bytes=30 << 20

time: 147 us -> 140 us (0.952)
  Pallas kernels: 138 us -> 130 us
    pallas_call x1, Pallas kernels: 47.5 us -> 41.2 us  [scatter_grads(): pl.pallas_call(scatter_kernel, out_shape=(jax.ShapeDtypeStruct((rows, 2,...]
    pallas_call x1, Pallas kernels: 41.5 us -> 39.7 us  [gather_relations(): pl.pallas_call(gather_kernel, out_shape=(jax.ShapeDtypeStruct((owners, pe...]
where the time goes in v5:
time: 140 us; the launch traced here: 139 us
  Pallas kernels  130 us (93%)
  local copies, waits for them, and re-layouts  8.31 us (6%)
    pallas_call x1, Pallas kernels, scatter_grads(): pl.pallas_call(scatter_kernel, out_shape=(jax.ShapeDtypeStruct((rows, 2,...  41.2 us
    pallas_call x1, Pallas kernels, gather_relations(): pl.pallas_call(gather_kernel, out_shape=(jax.ShapeDtypeStruct((owners, pe...  39.7 us
    pallas_call x1, Pallas kernels, run_stops(): pl.pallas_call(stops_kernel, out_shape=(jax.ShapeDtypeStruct((part, width...  32.7 us
    pallas_call x1, Pallas kernels, make_grads(): pl.pallas_call(group_grads, out_shape=(jax.ShapeDtypeStruct(grads.shape,...  10.8 us
    unnamed x15, local copies, waits for them, and re-layouts  8.2 us
    pallas_call x1, Pallas kernels, make_queries(): pl.pallas_call(group_queries, out_shape=jax.ShapeDtypeStruct(rows.shape,...  5.73 us

profile of v5, /device:TPU:0, one launch (start us, length us, event | category | flops | bytes accessed | tf_op | source)
XLA Modules:
  0.0 139.2 jit_solution(1005285884995161710)
XLA Ops:
  0.6 0.0 copy-start
  0.6 1.6 %copy-done = bf16[2048,512]{1,0:T(8,128)(2,1)S(1)} copy-done((bf16[2048,512]{1,0:T(8,128)(2,1)S(1)}, bf16[2048,512]{1,0:T(8,128)(2,1)}, u32[]{:S(2)}) %copy-start) | copy-done | bytes 2097176
  2.2 0.0 copy-start.1
  2.2 1.2 copy-done.1
  3.4 0.0 copy-start.2
  3.5 1.2 copy-done.2
  4.7 0.0 copy-start.4
  4.7 0.7 copy-done.4
  5.4 0.0 copy-start.5
  5.4 0.7 copy-done.5
  6.1 39.7 %gather_relations.1 = (bf16[8,2,512,512]{3,2,1,0:T(8,128)(2,1)S(1)}, bf16[2320,512]{1,0:T(8,128)(2,1)S(1)}, s32[8,64,2048]{2,1,0:T(8,128)S(1)}, s32[1,2048]{1,0:T(1,128)S(1)}, s32[16,128]{1,0:T(8,128)S(1)}) custom-call(bf16[2,512,512]{2,1,0:T(8,128)(2,1)S(1)} %copy-done.1, s32[1,2048]{1,0:T(1,128)S(1)} %bitcast.9, bf16[2048,512]{1,0:T(8,128)(2,1)S(1)} %copy-done, ...), custom_call_target="tpu_custom_call" | custom-call | tf_op jit(solution)/shard_map/gather_relations/pallas_call | solution.py:402
  45.8 0.1 slice_reduce_fusion
  45.9 0.1 pad_add_fusion.starts
  46.0 0.0 copy-start.3
  46.0 5.7 %make_queries.1.q = bf16[2320,512]{1,0:T(8,128)(2,1)S(1)} custom-call(s32[17]{0:T(128)S(1)} %pad_add_fusion.starts, bf16[2320,512]{1,0:T(8,128)(2,1)S(1)} %get-tuple-element.15.rows_ref, bf16[16,512,512]{2,1,0:T(8,128)(2,1)S(1)} %bitcast.5), custom_call_target="tpu_custom_call" | custom-call | tf_op jit(solution)/shard_map/make_queries/pallas_call | solution.py:127
  51.7 0.0 copy-done.3
  51.7 32.7 %run_stops.1 = (f32[256,512]{1,0:T(8,128)S(1)}, bf16[2320,512]{1,0:T(8,128)(2,1)S(1)}) custom-call(bf16[2320,512]{1,0:T(8,128)(2,1)S(1)} %make_queries.1.q, s32[8,64,2048]{2,1,0:T(8,128)S(1)} %get-tuple-element.17.packed, f32[256,512]{1,0:T(8,128)S(1)} %copy-done.3), custom_call_target="tpu_custom_call" | custom-call | tf_op jit(solution)/shard_map/run_stops/pallas_call | solution.py:573
  84.4 10.8 %make_grads.1 = (bf16[2320,512]{1,0:T(8,128)(2,1)S(1)}, bf16[2,8,512,512]{3,2,1,0:T(8,128)(2,1)S(1)}) custom-call(s32[17]{0:T(128)S(1)} %pad_add_fusion.starts, bf16[2320,512]{1,0:T(8,128)(2,1)S(1)} %get-tuple-element.15.rows_ref, bf16[2320,512]{1,0:T(8,128)(2,1)S(1)} %get-tuple-element.20.grads, bf16[16,512,512]{2,1,0:T(8,128)(2,1)S(1)} %bitcast.6), custom_call_target="tpu_custom_call" | custom-call | tf_op jit(solution)/shard_map/make_grads/pallas_call | solution.py:157
  95.2 41.2 %scatter_grads.1 = (f32[32,2,512]{2,1,0:T(2,128)S(1)}, bf16[2048,512]{1,0:T(8,128)(2,1)S(1)}) custom-call(s32[1,2048]{1,0:T(1,128)S(1)} %get-tuple-element.19.place, bf16[2,2,4,2,4,2,32,512]{7,6,5,4,3,2,1,0:T(8,128)(2,1)S(1)} %bitcast.7, bf16[2320,512]{1,0:T(8,128)(2,1)S(1)} %get-tuple-element.22.back), custom_call_target="tpu_custom_call" | custom-call | tf_op jit(solution)/shard_map/scatter_grads/pallas_call | solution.py:808
  136.4 0.8 copy.12
  137.2 1.3 copy.13
  138.6 0.7 copy.14
Async XLA Ops:
  0.6 1.6 %copy-start = (bf16[2048,512]{1,0:T(8,128)(2,1)S(1)}, bf16[2048,512]{1,0:T(8,128)(2,1)}, u32[]{:S(2)}) copy-start(bf16[2048,512]{1,0:T(8,128)(2,1)} %rows_in.1) | copy-start | bytes 6291460
  2.2 1.2 copy-start.1
  3.4 1.2 copy-start.2
  4.7 0.7 copy-start.4
  5.4 0.7 copy-start.5
  46.0 5.7 %copy-start.3 = (f32[256,512]{1,0:T(8,128)S(1)}, f32[256,512]{1,0:T(8,128)}, u32[]{:S(2)}) copy-start(f32[256,512]{1,0:T(8,128)} %entities.1) | copy-start | bytes 1572868

commit v6 on v5

--- a/solution.py
+++ b/solution.py
@@ -106,12 +106,14 @@
     pos_out[:, here] = meta[named : named + 1] * part + meta[named + 1 : named + 2]
 
 
+TOGETHER = 4
+
+
 def group_queries(starts, rows_ref, matrix, out):
-    k = pl.program_id(0)
-    window = out_window(starts, k)
-    rows = rows_ref[window[0], :]
-    new = jnp.dot(rows, matrix[0], preferred_element_type=F32).astype(BF)
-    out[window[0], :] = jnp.where(window[1], new, out[window[0], :])
+    for r in range(TOGETHER):
+        window, inside = out_window(starts, TOGETHER * pl.program_id(0) + r)
+        new = jnp.dot(rows_ref[window, :], matrix[r], preferred_element_type=F32).astype(BF)
+        out[window, :] = jnp.where(inside, new, out[window, :])
 
 
 def out_window(starts, k):
@@ -129,20 +131,27 @@
         out_shape=jax.ShapeDtypeStruct(rows.shape, BF),
         grid_spec=pltpu.PrefetchScalarGridSpec(
             num_scalar_prefetch=1,
-            grid=(nrel,),
+            grid=(nrel // TOGETHER,),
             in_specs=[
                 pl.BlockSpec(rows.shape, lambda k, s: (0, 0)),
-                pl.BlockSpec((1, width, width), lambda k, s: (k, 0, 0)),
+                pl.BlockSpec((TOGETHER, width, width), lambda k, s: (k, 0, 0)),
             ],
             out_specs=pl.BlockSpec(rows.shape, lambda k, s: (0, 0)),
         ),
-        compiler_params=pltpu.CompilerParams(vmem_limit_bytes=20 << 20),
+        compiler_params=pltpu.CompilerParams(vmem_limit_bytes=16 << 20),
         name="make_queries",
     )(starts, rows, matrices)
 
 
-def group_grads(starts, rows_ref, grads, matrix, back, terms):
-    window, inside = out_window(starts, pl.program_id(0))
+def group_grads(starts, rows_ref, grads, matrix, state, back, terms, state_out, sem):
+    step = pl.program_id(0)
+    keep = pltpu.make_async_copy(state, state_out, sem)
+
+    @pl.when(step == 0)
+    def _():
+        keep.start()
+
+    window, inside = out_window(starts, step)
     grad = grads[window, :]
     new = lax.dot_general(grad, matrix[0], (((1,), (1,)), ((), ())), preferred_element_type=F32).astype(BF)
     back[window, :] = jnp.where(inside, new, back[window, :])
@@ -150,8 +159,12 @@
     rows = jnp.where(inside, rows, jnp.zeros_like(rows))
     terms[0, 0] = lax.dot_general(rows, grad, (((0,), (0,)), ((), ())), preferred_element_type=F32).astype(BF)
 
-
-def make_grads(starts, rows, grads, matrices):
+    @pl.when(step == pl.num_programs(0) - 1)
+    def _():
+        keep.wait()
+
+
+def make_grads(starts, rows, grads, matrices, state):
     nrel, width, _ = matrices.shape
     whole = pl.BlockSpec(grads.shape, lambda k, s: (0, 0))
     return pl.pallas_call(
@@ -159,19 +172,27 @@
         out_shape=(
             jax.ShapeDtypeStruct(grads.shape, BF),
             jax.ShapeDtypeStruct((2, nrel // 2, width, width), BF),
+            jax.ShapeDtypeStruct(state.shape, F32),
         ),
         grid_spec=pltpu.PrefetchScalarGridSpec(
             num_scalar_prefetch=1,
             grid=(nrel,),
-            in_specs=[whole, whole, pl.BlockSpec((1, width, width), lambda k, s: (k, 0, 0))],
+            in_specs=[
+                whole,
+                whole,
+                pl.BlockSpec((1, width, width), lambda k, s: (k, 0, 0)),
+                pl.BlockSpec(memory_space=pl.ANY),
+            ],
             out_specs=(
                 whole,
                 pl.BlockSpec((1, 1, width, width), lambda k, s: (lax.rem(k, 2), k // 2, 0, 0)),
+                pl.BlockSpec(memory_space=pl.ANY),
             ),
+            scratch_shapes=[pltpu.SemaphoreType.DMA],
         ),
-        compiler_params=pltpu.CompilerParams(vmem_limit_bytes=20 << 20),
+        compiler_params=pltpu.CompilerParams(vmem_limit_bytes=16 << 20),
         name="make_grads",
-    )(starts, rows, grads, matrices)
+    )(starts, rows, grads, matrices, state)
 
 
 LOW = 64
@@ -426,7 +447,7 @@
             collective_id=0, has_side_effects=True, vmem_limit_bytes=24 << 20
         ),
         name="gather_relations",
-    )(relations, ids, rows, picks, target)
+    )(*(pltpu.with_memory_space_constraint(v, pltpu.HBM) for v in (relations, ids, rows, picks, target)))
     matrices, rows, packed, place, starts = out
     starts = jnp.concatenate([starts[:, 0], jnp.full((1,), total, jnp.int32)])
     return matrices.reshape(nrel, width, width), rows, packed, place, starts
@@ -777,15 +798,16 @@
         joined(j)
         for unit in units[j]:
             unit.one()
-    unsort(0, 3)
+    unsort(0, 4)
     for phase in range(3):
-        for unit in every:
+        for u, unit in enumerate(every):
             unit.two()
-        unsort(3 + 4 * phase, 5 + 4 * phase)
-        for unit in every:
+            if u % 4 == 3:
+                unsort(4 + 4 * phase + u // 4, 5 + 4 * phase + u // 4)
+        for u, unit in enumerate(every):
             unit.three()
-        unsort(5 + 4 * phase, 7 + 4 * phase)
-    unsort(15, 16)
+            if u % 4 == 3:
+                unsort(6 + 4 * phase + u // 4, 7 + 4 * phase + u // 4)
     for j in range(2):
         for u, unit in enumerate(units[j]):
             out[unit.row[0] : unit.row[0] + rows, j, unit.column[0] : unit.column[0] + columns] = unit.result()
@@ -841,7 +863,7 @@
     )
     queries = make_queries(starts, sorted_rows, matrices)
     state, query_grad = run_stops(queries, packed, entities)
-    back, terms = make_grads(starts, sorted_rows, query_grad, matrices)
+    back, terms, state = make_grads(starts, sorted_rows, query_grad, matrices, state)
     relation_grad, source_grad = scatter_grads(place, terms, back)
     return (state, source_grad, relation_grad)
 

time: 140 us -> 129 us (0.921)
  local copies, waits for them, and re-layouts: 8.31 us -> 2.09 us
  Pallas kernels: 130 us -> 126 us
    unnamed x15 -> x4, local copies, waits for them, and re-layouts: 8.2 us -> 1.98 us
    pallas_call x1, Pallas kernels: 5.73 us -> 3.63 us  [make_queries(): pl.pallas_call(group_queries, out_shape=jax.ShapeDtypeStruct(rows.shape,...]
    pallas_call x1, Pallas kernels: 41.2 us -> 39.5 us  [scatter_grads(): pl.pallas_call(scatter_kernel, out_shape=(jax.ShapeDtypeStruct((rows, 2,...]
where the time goes in v6:
time: 129 us
  Pallas kernels  126 us (98%)
  local copies, waits for them, and re-layouts  2.09 us (2%)
    pallas_call x1, Pallas kernels, gather_relations(): pl.pallas_call(gather_kernel, out_shape=(jax.ShapeDtypeStruct((owners, pe...  39.5 us
    pallas_call x1, Pallas kernels, scatter_grads(): pl.pallas_call(scatter_kernel, out_shape=(jax.ShapeDtypeStruct((rows, 2,...  39.5 us
    pallas_call x1, Pallas kernels, run_stops(): pl.pallas_call(stops_kernel, out_shape=(jax.ShapeDtypeStruct((part, width...  32.7 us
    pallas_call x1, Pallas kernels, make_grads(): pl.pallas_call(group_grads, out_shape=(jax.ShapeDtypeStruct(grads.shape,...  10.8 us
    pallas_call x1, Pallas kernels, make_queries(): pl.pallas_call(group_queries, out_shape=jax.ShapeDtypeStruct(rows.shape,...  3.63 us

profile of v6, /device:TPU:0, one launch (start us, length us, event | category | flops | bytes accessed | tf_op | source)
XLA Modules:
  0.0 129.0 jit_solution(15015340977641914759)
XLA Ops:
  0.6 39.5 %gather_relations.1 = (bf16[8,2,512,512]{3,2,1,0:T(8,128)(2,1)S(1)}, bf16[2320,512]{1,0:T(8,128)(2,1)S(1)}, s32[8,64,2048]{2,1,0:T(8,128)S(1)}, s32[1,2048]{1,0:T(1,128)S(1)}, s32[16,128]{1,0:T(8,128)S(1)}) custom-call(bf16[2,512,512]{2,1,0:T(8,128)(2,1)} %own_in.1, s32[1,2048]{1,0:T(1,128)} %bitcast.9, bf16[2048,512]{1,0:T(8,128)(2,1)} %rows_in.1, ...), custom_call_target="tpu_custom_call" | custom-call | tf_op jit(solution)/shard_map/gather_relations/pallas_call | solution.py:423
  40.2 0.1 slice_reduce_fusion
  40.3 0.1 pad_add_fusion.starts
  40.4 0.0 copy-start
  40.4 3.6 %make_queries.1.q = bf16[2320,512]{1,0:T(8,128)(2,1)S(1)} custom-call(s32[17]{0:T(128)S(1)} %pad_add_fusion.starts, bf16[2320,512]{1,0:T(8,128)(2,1)S(1)} %get-tuple-element.16.rows_ref, bf16[16,512,512]{2,1,0:T(8,128)(2,1)S(1)} %bitcast.5), custom_call_target="tpu_custom_call" | custom-call | tf_op jit(solution)/shard_map/make_queries/pallas_call | solution.py:129
  44.0 0.0 copy-done
  44.0 32.7 %run_stops.1 = (f32[256,512]{1,0:T(8,128)S(1)}, bf16[2320,512]{1,0:T(8,128)(2,1)S(1)}) custom-call(bf16[2320,512]{1,0:T(8,128)(2,1)S(1)} %make_queries.1.q, s32[8,64,2048]{2,1,0:T(8,128)S(1)} %get-tuple-element.18.packed, f32[256,512]{1,0:T(8,128)S(1)} %copy-done), custom_call_target="tpu_custom_call" | custom-call | tf_op jit(solution)/shard_map/run_stops/pallas_call | solution.py:594
  76.7 10.8 %make_grads.1 = (bf16[2320,512]{1,0:T(8,128)(2,1)S(1)}, bf16[2,8,512,512]{3,2,1,0:T(8,128)(2,1)S(1)}, f32[256,512]{1,0:T(8,128)}) custom-call(s32[17]{0:T(128)S(1)} %pad_add_fusion.starts, bf16[2320,512]{1,0:T(8,128)(2,1)S(1)} %get-tuple-element.16.rows_ref, bf16[2320,512]{1,0:T(8,128)(2,1)S(1)} %get-tuple-element.19.grads, ...), custom_call_target="tpu_custom_call" | custom-call | tf_op jit(solution)/shard_map/make_grads/pallas_call | solution.py:170
  87.5 39.5 %scatter_grads.1 = (f32[32,2,512]{2,1,0:T(2,128)S(1)}, bf16[2048,512]{1,0:T(8,128)(2,1)S(1)}) custom-call(s32[1,2048]{1,0:T(1,128)S(1)} %get-tuple-element.22.place, bf16[2,2,4,2,4,2,32,512]{7,6,5,4,3,2,1,0:T(8,128)(2,1)S(1)} %bitcast.7, bf16[2320,512]{1,0:T(8,128)(2,1)S(1)} %get-tuple-element.24.back), custom_call_target="tpu_custom_call" | custom-call | tf_op jit(solution)/shard_map/scatter_grads/pallas_call | solution.py:830
  127.0 1.3 %copy.11 = bf16[2048,512]{1,0:T(8,128)(2,1)} copy(bf16[2048,512]{1,0:T(8,128)(2,1)S(1)} %get-tuple-element.31) | data formatting | bytes 4194304
  128.4 0.7 copy.12
Async XLA Ops:
  40.4 3.6 %copy-start = (f32[256,512]{1,0:T(8,128)S(1)}, f32[256,512]{1,0:T(8,128)}, u32[]{:S(2)}) copy-start(f32[256,512]{1,0:T(8,128)} %entities.1) | copy-start | bytes 1572868

commit v7 on v6

--- a/solution.py
+++ b/solution.py
@@ -143,6 +143,9 @@
     )(starts, rows, matrices)
 
 
+PAIR = 2
+
+
 def group_grads(starts, rows_ref, grads, matrix, state, back, terms, state_out, sem):
     step = pl.program_id(0)
     keep = pltpu.make_async_copy(state, state_out, sem)
@@ -151,13 +154,14 @@
     def _():
         keep.start()
 
-    window, inside = out_window(starts, step)
-    grad = grads[window, :]
-    new = lax.dot_general(grad, matrix[0], (((1,), (1,)), ((), ())), preferred_element_type=F32).astype(BF)
-    back[window, :] = jnp.where(inside, new, back[window, :])
-    rows = rows_ref[window, :]
-    rows = jnp.where(inside, rows, jnp.zeros_like(rows))
-    terms[0, 0] = lax.dot_general(rows, grad, (((0,), (0,)), ((), ())), preferred_element_type=F32).astype(BF)
+    for r in range(PAIR):
+        window, inside = out_window(starts, PAIR * step + r)
+        grad = grads[window, :]
+        rows = rows_ref[window, :]
+        rows = jnp.where(inside, rows, jnp.zeros_like(rows))
+        terms[r, 0] = lax.dot_general(rows, grad, (((0,), (0,)), ((), ())), preferred_element_type=F32).astype(BF)
+        new = lax.dot_general(grad, matrix[r], (((1,), (1,)), ((), ())), preferred_element_type=F32).astype(BF)
+        back[window, :] = jnp.where(inside, new, back[window, :])
 
     @pl.when(step == pl.num_programs(0) - 1)
     def _():
@@ -176,16 +180,16 @@
         ),
         grid_spec=pltpu.PrefetchScalarGridSpec(
             num_scalar_prefetch=1,
-            grid=(nrel,),
+            grid=(nrel // PAIR,),
             in_specs=[
                 whole,
                 whole,
-                pl.BlockSpec((1, width, width), lambda k, s: (k, 0, 0)),
+                pl.BlockSpec((PAIR, width, width), lambda k, s: (k, 0, 0)),
                 pl.BlockSpec(memory_space=pl.ANY),
             ],
             out_specs=(
                 whole,
-                pl.BlockSpec((1, 1, width, width), lambda k, s: (lax.rem(k, 2), k // 2, 0, 0)),
+                pl.BlockSpec((PAIR, 1, width, width), lambda k, s: (0, k, 0, 0)),
                 pl.BlockSpec(memory_space=pl.ANY),
             ),
             scratch_shapes=[pltpu.SemaphoreType.DMA],

time: 129 us -> 128 us (level)
  no operation moved by 1% of the time
where the time goes in v7:
time: 128 us
  Pallas kernels  125 us (98%)
  local copies, waits for them, and re-layouts  2.09 us (2%)
    pallas_call x1, Pallas kernels, gather_relations(): pl.pallas_call(gather_kernel, out_shape=(jax.ShapeDtypeStruct((owners, pe...  39.5 us
    pallas_call x1, Pallas kernels, scatter_grads(): pl.pallas_call(scatter_kernel, out_shape=(jax.ShapeDtypeStruct((rows, 2,...  39.5 us
    pallas_call x1, Pallas kernels, run_stops(): pl.pallas_call(stops_kernel, out_shape=(jax.ShapeDtypeStruct((part, width...  32.7 us
    pallas_call x1, Pallas kernels, make_grads(): pl.pallas_call(group_grads, out_shape=(jax.ShapeDtypeStruct(grads.shape,...  9.77 us
    pallas_call x1, Pallas kernels, make_queries(): pl.pallas_call(group_queries, out_shape=jax.ShapeDtypeStruct(rows.shape,...  3.63 us

profile of v7, /device:TPU:0, one launch (start us, length us, event | category | flops | bytes accessed | tf_op | source)
XLA Modules:
  0.0 127.9 jit_solution(8027570375495220400)
XLA Ops:
  0.6 39.5 %gather_relations.1 = (bf16[8,2,512,512]{3,2,1,0:T(8,128)(2,1)S(1)}, bf16[2320,512]{1,0:T(8,128)(2,1)S(1)}, s32[8,64,2048]{2,1,0:T(8,128)S(1)}, s32[1,2048]{1,0:T(1,128)S(1)}, s32[16,128]{1,0:T(8,128)S(1)}) custom-call(bf16[2,512,512]{2,1,0:T(8,128)(2,1)} %own_in.1, s32[1,2048]{1,0:T(1,128)} %bitcast.9, bf16[2048,512]{1,0:T(8,128)(2,1)} %rows_in.1, ...), custom_call_target="tpu_custom_call" | custom-call | tf_op jit(solution)/shard_map/gather_relations/pallas_call | solution.py:427
  40.2 0.1 slice_reduce_fusion
  40.3 0.1 pad_add_fusion.starts
  40.4 0.0 copy-start
  40.4 3.6 %make_queries.1.q = bf16[2320,512]{1,0:T(8,128)(2,1)S(1)} custom-call(s32[17]{0:T(128)S(1)} %pad_add_fusion.starts, bf16[2320,512]{1,0:T(8,128)(2,1)S(1)} %get-tuple-element.16.rows_ref, bf16[16,512,512]{2,1,0:T(8,128)(2,1)S(1)} %bitcast.5), custom_call_target="tpu_custom_call" | custom-call | tf_op jit(solution)/shard_map/make_queries/pallas_call | solution.py:129
  44.0 0.0 copy-done
  44.0 32.7 %run_stops.1 = (f32[256,512]{1,0:T(8,128)S(1)}, bf16[2320,512]{1,0:T(8,128)(2,1)S(1)}) custom-call(bf16[2320,512]{1,0:T(8,128)(2,1)S(1)} %make_queries.1.q, s32[8,64,2048]{2,1,0:T(8,128)S(1)} %get-tuple-element.18.packed, f32[256,512]{1,0:T(8,128)S(1)} %copy-done), custom_call_target="tpu_custom_call" | custom-call | tf_op jit(solution)/shard_map/run_stops/pallas_call | solution.py:598
  76.7 9.8 %make_grads.1 = (bf16[2320,512]{1,0:T(8,128)(2,1)S(1)}, bf16[2,8,512,512]{3,2,1,0:T(8,128)(2,1)S(1)}, f32[256,512]{1,0:T(8,128)}) custom-call(s32[17]{0:T(128)S(1)} %pad_add_fusion.starts, bf16[2320,512]{1,0:T(8,128)(2,1)S(1)} %get-tuple-element.16.rows_ref, bf16[2320,512]{1,0:T(8,128)(2,1)S(1)} %get-tuple-element.19.grads, ...), custom_call_target="tpu_custom_call" | custom-call | tf_op jit(solution)/shard_map/make_grads/pallas_call | solution.py:174
  86.5 39.5 %scatter_grads.1 = (f32[32,2,512]{2,1,0:T(2,128)S(1)}, bf16[2048,512]{1,0:T(8,128)(2,1)S(1)}) custom-call(s32[1,2048]{1,0:T(1,128)S(1)} %get-tuple-element.22.place, bf16[2,2,4,2,4,2,32,512]{7,6,5,4,3,2,1,0:T(8,128)(2,1)S(1)} %bitcast.7, bf16[2320,512]{1,0:T(8,128)(2,1)S(1)} %get-tuple-element.24.back), custom_call_target="tpu_custom_call" | custom-call | tf_op jit(solution)/shard_map/scatter_grads/pallas_call | solution.py:834
  125.9 1.3 %copy.11 = bf16[2048,512]{1,0:T(8,128)(2,1)} copy(bf16[2048,512]{1,0:T(8,128)(2,1)S(1)} %get-tuple-element.31) | data formatting | bytes 4194304
  127.3 0.7 copy.12
Async XLA Ops:
  40.4 3.6 %copy-start = (f32[256,512]{1,0:T(8,128)S(1)}, f32[256,512]{1,0:T(8,128)}, u32[]{:S(2)}) copy-start(f32[256,512]{1,0:T(8,128)} %entities.1) | copy-start | bytes 1572868

commit v8 on v7

--- a/solution.py
+++ b/solution.py
@@ -670,7 +670,7 @@
     shapes = []
     for phase in range(3):
         half, whole = piece_shape(order, phase, rows, columns)
-        shapes += [(2, *half), (2, *whole)]
+        shapes += [(2, *half), (2, *whole)] if phase < 2 else [(3, *whole)]
     return shapes
 
 
@@ -700,15 +700,26 @@
         t = turn(getattr(self.at, axis), by)
         return {**self.fixed, **({"zh": t // 2, "zl": lax.rem(t, 2)} if axis == "z" else {axis: t})}
 
+    def straight(self):
+        self.whole = self.landings[-1]
+        self.f = [
+            self.mail.send(self.view(self.spot(by)), self.whole.at[i], device)
+            for i, (by, device) in enumerate(zip((1, 3, 2), self.ways[self.order[2]]))
+        ]
+
     def one(self):
+        if self.phase == 2:
+            return self.straight()
         self.half, self.whole = self.landings[2 * self.phase : 2 * self.phase + 2]
-        self.devices = self.ways[self.order[self.phase]]
+        self.devices = self.ways[self.order[self.phase]][:2]
         self.h = [
             self.mail.send(self.view(self.spot(2), d), self.half.at[d], device)
             for d, device in enumerate(self.devices)
         ]
 
     def two(self):
+        if self.phase == 2:
+            return
         self.f = []
         for d, device in enumerate(self.devices):
             self.h[d].wait_recv()
@@ -727,7 +738,7 @@
 
     def result(self):
         own = self.view(self.fixed)[...].astype(F32)
-        return own + self.whole[0].astype(F32) + self.whole[1].astype(F32)
+        return own + self.whole[0].astype(F32) + self.whole[1].astype(F32) + self.whole[2].astype(F32)
 
 
 def scatter_kernel(place, terms, back, out, source_grad, got, *rest):
@@ -737,9 +748,9 @@
     mail = Mail(send_sem, recv_sem)
     partner = at.device(core=1 - at.core)
     ways = {
-        "x": (at.device(x=turn(at.x, 1)), at.device(x=turn(at.x, 3))),
-        "y": (at.device(y=turn(at.y, 1)), at.device(y=turn(at.y, 3))),
-        "z": (at.device(z=turn(at.z, 1)), at.device(z=turn(at.z, 3))),
+        "x": tuple(at.device(x=turn(at.x, by)) for by in (1, 3, 2)),
+        "y": tuple(at.device(y=turn(at.y, by)) for by in (1, 3, 2)),
+        "z": tuple(at.device(z=turn(at.z, by)) for by in (1, 3, 2)),
     }
     greet([partner, *ways["x"], *ways["y"], *ways["z"]])
 
@@ -791,7 +802,7 @@
         [
             Eighth(
                 mail, at, got.at[j], (u // 2 * rows, rows), (u % 2 * columns, columns), ORDERS[j][u],
-                landings[(4 * j + u) * 6 : (4 * j + u) * 6 + 6], ways,
+                landings[(4 * j + u) * 5 : (4 * j + u) * 5 + 5], ways,
             )
             for u in range(4)
         ]
@@ -846,8 +857,8 @@
             ),
             pltpu.SemaphoreType.DMA((2, 8)),
             pltpu.SemaphoreType.DMA((2, 8)),
-            pltpu.SemaphoreType.DMA((96,)),
-            pltpu.SemaphoreType.DMA((96,)),
+            pltpu.SemaphoreType.DMA((88,)),
+            pltpu.SemaphoreType.DMA((88,)),
         ],
         compiler_params=pltpu.CompilerParams(
             collective_id=1, has_side_effects=True, vmem_limit_bytes=30 << 20

time: 128 us -> 126 us (0.984)
  Pallas kernels: 125 us -> 122 us
    pallas_call x1, Pallas kernels: 39.5 us -> 36.4 us  [scatter_grads(): pl.pallas_call(scatter_kernel, out_shape=(jax.ShapeDtypeStruct((rows, 2,...]
where the time goes in v8:
time: 126 us; the launch traced here: 125 us
  Pallas kernels  122 us (97%)
  local copies, waits for them, and re-layouts  2.09 us (2%)
    pallas_call x1, Pallas kernels, gather_relations(): pl.pallas_call(gather_kernel, out_shape=(jax.ShapeDtypeStruct((owners, pe...  39.5 us
    pallas_call x1, Pallas kernels, scatter_grads(): pl.pallas_call(scatter_kernel, out_shape=(jax.ShapeDtypeStruct((rows, 2,...  36.4 us
    pallas_call x1, Pallas kernels, run_stops(): pl.pallas_call(stops_kernel, out_shape=(jax.ShapeDtypeStruct((part, width...  32.7 us
    pallas_call x1, Pallas kernels, make_grads(): pl.pallas_call(group_grads, out_shape=(jax.ShapeDtypeStruct(grads.shape,...  9.77 us
    pallas_call x1, Pallas kernels, make_queries(): pl.pallas_call(group_queries, out_shape=jax.ShapeDtypeStruct(rows.shape,...  3.63 us

profile of v8, /device:TPU:0, one launch (start us, length us, event | category | flops | bytes accessed | tf_op | source)
XLA Modules:
  0.0 124.8 jit_solution(10629869574280010426)
XLA Ops:
  0.6 39.5 %gather_relations.1 = (bf16[8,2,512,512]{3,2,1,0:T(8,128)(2,1)S(1)}, bf16[2320,512]{1,0:T(8,128)(2,1)S(1)}, s32[8,64,2048]{2,1,0:T(8,128)S(1)}, s32[1,2048]{1,0:T(1,128)S(1)}, s32[16,128]{1,0:T(8,128)S(1)}) custom-call(bf16[2,512,512]{2,1,0:T(8,128)(2,1)} %own_in.1, s32[1,2048]{1,0:T(1,128)} %bitcast.9, bf16[2048,512]{1,0:T(8,128)(2,1)} %rows_in.1, ...), custom_call_target="tpu_custom_call" | custom-call | tf_op jit(solution)/shard_map/gather_relations/pallas_call | solution.py:427
  40.2 0.1 slice_reduce_fusion
  40.3 0.1 pad_add_fusion.starts
  40.4 0.0 copy-start
  40.4 3.6 %make_queries.1.q = bf16[2320,512]{1,0:T(8,128)(2,1)S(1)} custom-call(s32[17]{0:T(128)S(1)} %pad_add_fusion.starts, bf16[2320,512]{1,0:T(8,128)(2,1)S(1)} %get-tuple-element.16.rows_ref, bf16[16,512,512]{2,1,0:T(8,128)(2,1)S(1)} %bitcast.5), custom_call_target="tpu_custom_call" | custom-call | tf_op jit(solution)/shard_map/make_queries/pallas_call | solution.py:129
  44.0 0.0 copy-done
  44.0 32.7 %run_stops.1 = (f32[256,512]{1,0:T(8,128)S(1)}, bf16[2320,512]{1,0:T(8,128)(2,1)S(1)}) custom-call(bf16[2320,512]{1,0:T(8,128)(2,1)S(1)} %make_queries.1.q, s32[8,64,2048]{2,1,0:T(8,128)S(1)} %get-tuple-element.18.packed, f32[256,512]{1,0:T(8,128)S(1)} %copy-done), custom_call_target="tpu_custom_call" | custom-call | tf_op jit(solution)/shard_map/run_stops/pallas_call | solution.py:598
  76.7 9.8 %make_grads.1 = (bf16[2320,512]{1,0:T(8,128)(2,1)S(1)}, bf16[2,8,512,512]{3,2,1,0:T(8,128)(2,1)S(1)}, f32[256,512]{1,0:T(8,128)}) custom-call(s32[17]{0:T(128)S(1)} %pad_add_fusion.starts, bf16[2320,512]{1,0:T(8,128)(2,1)S(1)} %get-tuple-element.16.rows_ref, bf16[2320,512]{1,0:T(8,128)(2,1)S(1)} %get-tuple-element.19.grads, ...), custom_call_target="tpu_custom_call" | custom-call | tf_op jit(solution)/shard_map/make_grads/pallas_call | solution.py:174
  86.5 36.4 %scatter_grads.1 = (f32[32,2,512]{2,1,0:T(2,128)S(1)}, bf16[2048,512]{1,0:T(8,128)(2,1)S(1)}) custom-call(s32[1,2048]{1,0:T(1,128)S(1)} %get-tuple-element.22.place, bf16[2,2,4,2,4,2,32,512]{7,6,5,4,3,2,1,0:T(8,128)(2,1)S(1)} %bitcast.7, bf16[2320,512]{1,0:T(8,128)(2,1)S(1)} %get-tuple-element.24.back), custom_call_target="tpu_custom_call" | custom-call | tf_op jit(solution)/shard_map/scatter_grads/pallas_call | solution.py:845
  122.8 1.3 %copy.11 = bf16[2048,512]{1,0:T(8,128)(2,1)} copy(bf16[2048,512]{1,0:T(8,128)(2,1)S(1)} %get-tuple-element.31) | data formatting | bytes 4194304
  124.1 0.7 copy.12
Async XLA Ops:
  40.4 3.6 %copy-start = (f32[256,512]{1,0:T(8,128)S(1)}, f32[256,512]{1,0:T(8,128)}, u32[]{:S(2)}) copy-start(f32[256,512]{1,0:T(8,128)} %entities.1) | copy-start | bytes 1572868
